TPU v7x, 128 devices: a whole 4x4x4 slice. The times are simulated.
128 devices in a mesh: row: 16 (over z, x), col: 8 (over y, core).
Axes of the slice: x: 4, y: 4, z: 4, core: 2. Of those that a mesh axis runs over, the one named last changes fastest.
Arguments:
- edge_vec: float32 [3, 1024], P(None, ('row', 'col')), may hold values from -8 to 8
- edge_atoms: int32 [2, 1024], P(None, ('row', 'col')), may hold values from 0 to 95
- block_weight: bfloat16 [144, 16384], replicated, may hold values from -0.5 to 0.5
- base_hamiltonian: bfloat16 [12288, 12288], P('row', 'col'), as said below
- lower_bound: float32 [1], replicated, may hold values from -50 to -40
- upper_bound: float32 [1], replicated, may hold values from 40 to 50
Outputs:
- purified: float32 [12288, 12288], P('row', 'col')
Inputs may be any that keep to these rules, and one draw needn't show every extreme that they name: `base_hamiltonian`: symmetric.
All inputs are finite; a program needn't handle non-finite values.
Results may differ from a plain program's by a relative error of at most 0.0031.
Values may be sent and summed in bfloat16 or wider, within the bound.
A program may use at most 192 MiB of HBM per device.

v0:
```python
import jax
import jax.numpy as jnp
from jax import lax
from jax.sharding import PartitionSpec as P

ORB = 128
NR = 16
RB = 6


def features(edge_vec):
    squared = jnp.sum(edge_vec * edge_vec, axis=0)
    radius = jnp.sqrt(squared + 0.25)
    unit_x = edge_vec[0] / radius
    unit_y = edge_vec[1] / radius
    unit_z = edge_vec[2] / radius
    harmonics = jnp.stack(
        [
            jnp.ones_like(unit_x),
            unit_x,
            unit_y,
            unit_z,
            unit_x * unit_y,
            unit_y * unit_z,
            unit_z * unit_x,
            unit_x * unit_x - unit_y * unit_y,
            3.0 * unit_z * unit_z - 1.0,
        ]
    )
    centers = 1.0 + 0.3 * jnp.arange(NR, dtype=jnp.float32)
    radial = jnp.exp(-jnp.square((radius[None, :] - centers[:, None]) / 0.5))
    return (radial[:, None, :] * harmonics[None, :, :]).reshape(NR * 9, edge_vec.shape[1])


def shards(edge_vec, edge_atoms, block_weight, base_hamiltonian, lower_bound, upper_bound):
    atoms_float = edge_atoms.astype(jnp.float32)
    packed = jnp.concatenate([features(edge_vec), atoms_float], axis=0)
    gathered = lax.all_gather(packed, ("row", "col"), axis=1, tiled=True)
    embedding = gathered[:-2]
    atom_pairs = gathered[-2:].astype(jnp.int32)
    first_atom = atom_pairs[0]
    second_atom = atom_pairs[1]
    atoms_total = RB * lax.axis_size("row")
    col_blocks = atoms_total // lax.axis_size("col")
    row_index = lax.axis_index("row")
    col_index = lax.axis_index("col")
    row_atoms = row_index * RB + jnp.arange(RB, dtype=jnp.int32)
    col_atoms = col_index * col_blocks + jnp.arange(col_blocks, dtype=jnp.int32)
    direct = (
        (
            (first_atom[None, None, :] == row_atoms[:, None, None])
            & (second_atom[None, None, :] == col_atoms[None, :, None])
        )
        .astype(jnp.float32)
        .reshape(RB * col_blocks, -1)
    )
    mirror = (
        (
            (first_atom[None, None, :] == col_atoms[None, :, None])
            & (second_atom[None, None, :] == row_atoms[:, None, None])
        )
        .astype(jnp.float32)
        .reshape(RB * col_blocks, -1)
    )
    contract = (((1,), (1,)), ((), ()))
    coefficient = lax.dot_general(
        direct, embedding, contract, precision=lax.Precision.HIGHEST
    ).astype(jnp.bfloat16)
    coefficient_back = lax.dot_general(
        mirror, embedding, contract, precision=lax.Precision.HIGHEST
    ).astype(jnp.bfloat16)
    blocks = jnp.dot(coefficient, block_weight, preferred_element_type=jnp.float32).reshape(
        RB, col_blocks, ORB, ORB
    )
    blocks_back = jnp.dot(
        coefficient_back, block_weight, preferred_element_type=jnp.float32
    ).reshape(RB, col_blocks, ORB, ORB)
    tile_rows = RB * ORB
    tile_cols = col_blocks * ORB
    hamiltonian = (
        (blocks + blocks_back.transpose(0, 1, 3, 2))
        .transpose(0, 2, 1, 3)
        .reshape(tile_rows, tile_cols)
    )
    hamiltonian = hamiltonian + base_hamiltonian.astype(jnp.float32)
    global_rows = row_index * tile_rows + jnp.arange(tile_rows, dtype=jnp.int32)
    global_cols = col_index * tile_cols + jnp.arange(tile_cols, dtype=jnp.int32)
    diagonal_mask = global_rows[:, None] == global_cols[None, :]
    shifted = jnp.where(diagonal_mask, upper_bound[0], jnp.float32(0.0)) - hamiltonian
    start_density = (shifted / (upper_bound[0] - lower_bound[0])).astype(jnp.bfloat16)
    row_strip = lax.all_gather(start_density, "col", axis=1, tiled=True)
    return jnp.dot(
        row_strip,
        lax.all_gather(start_density, "row", axis=0, tiled=True),
        preferred_element_type=jnp.float32,
    )


def solution(mesh):
    return jax.shard_map(
        shards,
        mesh=mesh,
        in_specs=(P(None, ("row", "col")), P(None, ("row", "col")), P(), P("row", "col"), P(), P()),
        out_specs=P("row", "col"),
        check_vma=False,
    )
```

profile of v0, /device:TPU:1, one launch (start us, length us, event | category | flops | bytes accessed | tf_op | source)
XLA Modules:
  0.0 437.2 jit_solution(4057055565434168536)
XLA Ops:
  6.5 0.7 multiply_reduce_fusion
  7.3 0.8 multiply_subtract_fusion
  9.4 0.8 fusion.6
  10.3 0.8 copy.14
  11.2 0.1 broadcast_multiply_fusion
  11.3 0.1 mul.81
  11.4 39.7 %all_gather.9 = f32[146,1024]{0,1:T(8,128)S(1)} all-gather(f32[146,8]{0,1:T(8,128)S(1)} %pad_maximum_fusion), channel_id=1, replica_groups=mesh['row'=16,'col'=8] {'row','col'}, dimensions={1}, use_global_device_ids=true | all-gather | bytes 602688 | tf_op jit(solution)/shard_map/all_gather | solution.py:38
  51.1 0.2 slice_convert_fusion
  51.3 0.5 slice_reduce_fusion.1
  51.9 0.1 broadcast_compare_fusion.1
  52.0 0.1 broadcast_and_fusion
  52.1 0.5 convolution_convert_fusion
  52.7 0.5 convolution_convert_fusion.1
  53.3 3.4 convolution_bitcast_fusion.1
  56.6 3.1 copy.17
  59.7 0.8 convolution_bitcast_fusion
  60.5 3.0 copy.18
  63.5 6.6 %copy.15 = f32[6,12,128,128]{2,1,3,0:T(8,128)} copy(f32[6,12,128,128]{3,2,1,0:T(8,128)} %bitcast.52) | data formatting | bytes 9437184 | tf_op jit(solution)/shard_map/reshape | solution.py:77
  70.1 7.3 %bitcast_add_fusion = f32[6,12,128,128]{3,1,2,0:T(8,128)S(1)} fusion(f32[6,12,128,128]{2,1,3,0:T(8,128)} %copy.15, f32[6,12,128,128]{3,2,1,0:T(8,128)} %bitcast.51), kind=kLoop, calls=%fused_computation | loop fusion | flops 1179648 | bytes 14155776 | tf_op jit(solution)/shard_map/add | solution.py:81
  77.3 4.2 fusion.2
  81.6 0.7 all-gather.5.cloned.1.call-update
  82.3 91.0 %all-gather.3.cloned.1.call-done = bf16[768,12288]{1,0:T(8,128)(2,1)} async-done(((bf16[768,1536]{1,0:T(8,128)(2,1)}), bf16[768,12288]{1,0:T(8,128)(2,1)}) %all-gather.3.cloned.1.call-update) | async-done | bytes 18874384 | tf_op jit(solution)/shard_map/all_gather | solution.py:91
  173.4 220.8 %all-gather.5.cloned.1.call-done = bf16[12288,1536]{1,0:T(8,128)(2,1)} async-done(((bf16[768,1536]{1,0:T(8,128)(2,1)}), bf16[12288,1536]{1,0:T(8,128)(2,1)}) %all-gather.5.cloned.1.call-update) | async-done | bytes 37748752 | tf_op jit(solution)/shard_map/all_gather | solution.py:94
  394.2 36.2 %fusion.8 = f32[768,1536]{1,0:T(8,128)} fusion(bf16[768,12288]{1,0:T(8,128)(2,1)} %all-gather.3.cloned.1.call-done, bf16[12288,1536]{1,0:T(8,128)(2,1)} %all-gather.5.cloned.1.call-done), kind=kOutput, calls=%fused_computation.42 | convolution fusion | flops 28991029248 | bytes 61341696 | tf_op jit(solution)/shard_map/dot_general | solution.py:92
  (26 shorter events, 0.6 us)
Async XLA Ops:
  6.5 166.9 %all-gather.3.cloned.1.call-start = ((), (), s32[]{:S(2)}) async-start(), calls=%async_computation | async-start | bytes 21233664 | tf_op jit(solution)/shard_map/all_gather | solution.py:91
  52.7 7.0 %slice-start = ((s8[4718592]{0:T(1024)(128)(4,1)}), s8[4194304]{0:T(1024)(128)(4,1)S(1)}, s32[]{:S(2)}) async-start(s8[4718592]{0:T(1024)(128)(4,1)} %bitcast.49), calls=%async_computation.2 | async-start | bytes 8388608
  53.2 6.5 %slice-start.1 = ((s8[4718592]{0:T(1024)(128)(4,1)}), s8[524288]{0:T(1024)(128)(4,1)S(1)}, s32[]{:S(2)}) async-start(s8[4718592]{0:T(1024)(128)(4,1)} %bitcast.49), calls=%async_computation.3 | async-start | bytes 1048576
  70.1 7.3 %copy-start = (bf16[768,1536]{1,0:T(8,128)(2,1)S(1)}, bf16[768,1536]{1,0:T(8,128)(2,1)}, u32[]{:S(2)}) copy-start(bf16[768,1536]{1,0:T(8,128)(2,1)} %param.9) | copy-start | bytes 7077892
  81.6 312.6 %all-gather.5.cloned.1.call-start = ((), (), s32[]{:S(2)}) async-start(), calls=%async_computation.1 | async-start | bytes 40108032 | tf_op jit(solution)/shard_map/all_gather | solution.py:94
Sparse Core Ops, SparseCore 0:
  81.7 91.6 all-gather.2
  175.5 218.6 all-gather.4
where the time goes:
time: 438 us; the launch traced here: 437 us
  waiting for transfers between devices  313 us (71%)
  matrix products  41.4 us (9%)
  blocking collectives  39.7 us (9%)
  between operations  14.8 us (3%)
  other arithmetic  14.5 us (3%)
  local copies, waits for them, and re-layouts  14.2 us (3%)
    all_gather x1, waiting for transfers between devices, shards(): lax.all_gather(start_density, 'row', axis=0, tiled=True)  221 us
    all_gather x1, waiting for transfers between devices, shards(): row_strip = lax.all_gather(start_density, 'col', axis=1, tiled=True)  91 us
    all_gather x1, blocking collectives, shards(): gathered = lax.all_gather(packed, ('row', 'col'), axis=1, tiled=True)  39.7 us
    dot_general x1, matrix products, shards(): jnp.dot(row_strip, lax.all_gather(start_density, 'row', axis=0, tiled=Tru...  36.2 us
  transfers between devices with their start and end apart: 2, of which 2 were waited for; matrix products, arithmetic and copies ran while one was open for 0% of the time, Pallas kernels for 0%

commit v1 on v0

--- a/solution.py
+++ b/solution.py
@@ -1,11 +1,313 @@
 import jax
 import jax.numpy as jnp
 from jax import lax
+from jax.experimental import pallas as pl
+from jax.experimental.pallas import tpu as pltpu
 from jax.sharding import PartitionSpec as P
 
 ORB = 128
 NR = 16
 RB = 6
+ROWS = 768
+COLS = 1536
+K = 3072
+NJ = 6
+JW = COLS // NJ
+HALF = ROWS // 2
+QUART = ROWS // 4
+MESH = pl.DeviceIdType.MESH
+
+
+def plan():
+    z_period, y_period, y_lead = 12.7, 19.0, 8.0
+    unit_us, out_us, lag = 1.6, 4.3, 2.0
+    events = []
+    for j in range(NJ):
+        if j == 0:
+            events.append((0.0, "b_own", j))
+        events.append((z_period * j + 5.7, "b_relay", j))
+        if j + 1 < NJ:
+            events.append((z_period * j + 5.8, "b_own", j + 1))
+        events.append((z_period * (j + 1) + 2.0, "b_done", j))
+    for p in range(4):
+        start = y_lead + y_period * p
+        if p == 0:
+            events.append((start, "a_own", p))
+        events.append((start + 8.0, "a_relay", p))
+        if p + 1 < 4:
+            events.append((start + 8.1, "a_own", p + 1))
+        events.append((start + 14.5, "a_fwd", p))
+        events.append((start + y_period + 1.5, "a_far", p))
+        events.append((start + y_period + 4.0, "a_done", p))
+    events.sort(key=lambda e: e[0])
+    order = []
+    now, link = 0.0, 0.0
+    a_ok, b_ok = set(), set()
+    arrive = {}
+    todo = [(p, j) for j in range(NJ) for p in (0, 2, 1, 3)]
+    while todo or events:
+        while events and events[0][0] <= now:
+            _, name, arg = events.pop(0)
+            order.append((name, arg))
+            if name == "a_done":
+                a_ok.add(arg)
+            if name == "b_done":
+                b_ok.add(arg)
+        best = None
+        wake = events[0][0] if events else 1e9
+        for p, j in todo:
+            if p not in a_ok or j not in b_ok:
+                continue
+            needs = {0: [], 1: [(0, j)], 2: [], 3: [(1, j), (2, j)]}[p]
+            if any(n not in arrive for n in needs):
+                continue
+            at = max([now] + [arrive[n] for n in needs])
+            if at <= now:
+                rank = (p == 3, j, {0: 0, 2: 1, 1: 2, 3: 3}[p])
+                if best is None or rank < best[0]:
+                    best = (rank, (p, j))
+            else:
+                wake = min(wake, at)
+        if best is None:
+            now = wake
+            continue
+        p, j = best[1]
+        todo.remove((p, j))
+        order.append(("unit", p, j))
+        now += unit_us
+        if p != 3:
+            link = max(link, now) + out_us
+            arrive[(p, j)] = link + lag
+    return order, now
+
+
+def square_kernel(
+    t_ref, o_ref, a, b, s0, s1, s2, rf, rp, rm, out,
+    a2_sem, al_sem, ar_sem, af_sem, sb_sem, bl_sem, br_sem, bf_sem, rf_sem, rp_sem, rm_sem,
+    a2_snd, a_snd, ay_snd, sb_snd, b_snd, x_snd, own_sem, o_sem,
+):
+    row = lax.axis_index("row")
+    col = lax.axis_index("col")
+    z, x, y, c = row // 4, row % 4, col // 2, col % 2
+    mod = lambda v: (v + 4) % 4
+    dev = lambda zz, xx, yy, cc: (zz * 4 + xx, yy * 2 + cc)
+    zr, zl = dev(mod(z + 1), x, y, c), dev(mod(z - 1), x, y, c)
+    yr, yl = dev(z, x, mod(y + 1), c), dev(z, x, mod(y - 1), c)
+    xr, xl = dev(z, mod(x + 1), y, c), dev(z, mod(x - 1), y, c)
+    sib = dev(z, x, y, 1 - c)
+
+    barrier = pltpu.get_barrier_semaphore()
+    partners = [zr, zl, yr, yl, sib] + [
+        dev(z, mod(x + d), y, cc) for d in (1, 2, 3) for cc in (0, 1)
+    ]
+    for partner in partners:
+        pl.semaphore_signal(barrier, inc=1, device_id=partner, device_id_type=MESH)
+    pl.semaphore_wait(barrier, len(partners))
+
+    pending = []
+
+    def remote(src, dst, snd, rcv, target):
+        return pltpu.make_async_remote_copy(
+            src_ref=src, dst_ref=dst, send_sem=snd, recv_sem=rcv,
+            device_id=target, device_id_type=MESH,
+        )
+
+    def push(src, dst, snd, rcv, target):
+        copy = remote(src, dst, snd, rcv, target)
+        copy.start()
+        pending.append((None, copy))
+
+    def arrived(dst, rcv):
+        remote(dst, dst, own_sem.at[1], rcv, sib).wait_recv()
+
+    def a2(r):
+        kk = mod(x - r)
+        active = (kk // 2) == c
+        cols = pl.ds(pl.multiple_of((kk % 2) * ROWS, ROWS), ROWS)
+        place = pl.ds(pl.multiple_of(y * ROWS, ROWS), ROWS)
+        for s in range(2):
+            for h in range(2):
+                p = {0: 3, 2: 0, 1: 1 + h, 3: 2 - h}[r]
+                rows = pl.ds(h * HALF + s * QUART, QUART)
+                src = t_ref.at[rows, cols]
+                dst = a.at[p, rows, place]
+                if r:
+                    copy = remote(src, dst, a2_snd.at[r, s, h], a2_sem.at[p, s], dev(z, kk, y, h))
+                    cond = active
+                    pl.when(cond)(copy.start)
+                    pending.append((cond, copy))
+                else:
+                    copy = remote(src, dst, a2_snd.at[r, s, h], a2_sem.at[p, s], sib)
+                    cond = active & (c != h)
+                    pl.when(cond)(copy.start)
+                    pending.append((cond, copy))
+                    local = pltpu.make_async_copy(src, dst, a2_sem.at[p, s])
+                    pl.when(active & (c == h))(local.start)
+
+    def a_piece(p, s, yy):
+        return a.at[
+            p,
+            pl.ds(pl.multiple_of(c * HALF + s * QUART, QUART), QUART),
+            pl.ds(pl.multiple_of(yy * ROWS, ROWS), ROWS),
+        ]
+
+    def a_half(p, yy, cc):
+        return a.at[
+            p,
+            pl.ds(pl.multiple_of(cc * HALF, HALF), HALF),
+            pl.ds(pl.multiple_of(yy * ROWS, ROWS), ROWS),
+        ]
+
+    def a_own(p):
+        arrived(a_piece(p, 0, y), a2_sem.at[p, 0])
+        push(a_piece(p, 0, y), a_piece(p, 0, y), ay_snd.at[p, 0], al_sem.at[p, 0], yr)
+        arrived(a_piece(p, 1, y), a2_sem.at[p, 1])
+        push(a_piece(p, 1, y), a_piece(p, 1, y), ay_snd.at[p, 1], ar_sem.at[p, 1], yl)
+        push(a_piece(p, 1, y), a_piece(p, 1, y), ay_snd.at[p, 2], al_sem.at[p, 1], yr)
+        push(a_piece(p, 0, y), a_piece(p, 0, y), ay_snd.at[p, 3], ar_sem.at[p, 0], yl)
+        push(a_half(p, y, c), a_half(p, y, c), sb_snd.at[p, 0], sb_sem.at[p, 0], sib)
+
+    def a_relay(p):
+        left, right = mod(y - 1), mod(y + 1)
+        arrived(a_piece(p, 0, left), al_sem.at[p, 0])
+        push(a_piece(p, 0, left), a_piece(p, 0, left), ay_snd.at[p, 4], af_sem.at[p, 0], yr)
+        arrived(a_piece(p, 1, right), ar_sem.at[p, 1])
+        push(a_piece(p, 1, right), a_piece(p, 1, right), ay_snd.at[p, 5], af_sem.at[p, 1], yl)
+
+    def a_fwd(p):
+        left, right = mod(y - 1), mod(y + 1)
+        arrived(a_piece(p, 1, left), al_sem.at[p, 1])
+        push(a_half(p, left, c), a_half(p, left, c), sb_snd.at[p, 1], sb_sem.at[p, 1], sib)
+        arrived(a_piece(p, 0, right), ar_sem.at[p, 0])
+        push(a_half(p, right, c), a_half(p, right, c), sb_snd.at[p, 2], sb_sem.at[p, 2], sib)
+
+    def a_far(p):
+        far = mod(y + 2)
+        arrived(a_piece(p, 0, far), af_sem.at[p, 0])
+        arrived(a_piece(p, 1, far), af_sem.at[p, 1])
+        push(a_half(p, far, c), a_half(p, far, c), sb_snd.at[p, 3], sb_sem.at[p, 3], sib)
+
+    def a_done(p):
+        for i, yy in enumerate((y, mod(y - 1), mod(y + 1), mod(y + 2))):
+            arrived(a_half(p, yy, 1 - c), sb_sem.at[p, i])
+
+    def b_piece(j, s, zz):
+        return b.at[pl.ds(pl.multiple_of(zz * ROWS + s * HALF, HALF), HALF), pl.ds(j * JW, JW)]
+
+    def b_own(j):
+        for i, (s, right) in enumerate(((0, True), (1, False), (1, True), (0, False))):
+            src = t_ref.at[pl.ds(s * HALF, HALF), pl.ds(j * JW, JW)]
+            rcv = bl_sem.at[j, s] if right else br_sem.at[j, s]
+            push(src, b_piece(j, s, z), b_snd.at[j, i], rcv, zr if right else zl)
+
+    def b_relay(j):
+        left, right = mod(z - 1), mod(z + 1)
+        arrived(b_piece(j, 0, left), bl_sem.at[j, 0])
+        push(b_piece(j, 0, left), b_piece(j, 0, left), b_snd.at[j, 4], bf_sem.at[j, 0], zr)
+        arrived(b_piece(j, 1, right), br_sem.at[j, 1])
+        push(b_piece(j, 1, right), b_piece(j, 1, right), b_snd.at[j, 5], bf_sem.at[j, 1], zl)
+
+    own_tile = b.at[pl.ds(pl.multiple_of(z * ROWS, ROWS), ROWS), :]
+    own_copy = pltpu.make_async_copy(t_ref, own_tile, own_sem.at[0])
+
+    def b_done(j):
+        if j == 0:
+            own_copy.wait()
+        arrived(b_piece(j, 1, mod(z - 1)), bl_sem.at[j, 1])
+        arrived(b_piece(j, 0, mod(z + 1)), br_sem.at[j, 0])
+        for s in range(2):
+            arrived(b_piece(j, s, mod(z + 2)), bf_sem.at[j, s])
+
+    def block(ref, j, h):
+        return ref.at[pl.ds(h * HALF, HALF), pl.ds(j * JW, JW)]
+
+    def unit(p, j):
+        cols = pl.ds(j * JW, JW)
+        if p == 1:
+            for h in range(2):
+                arrived(block(rf, j, h), rf_sem.at[j, h])
+        if p == 3:
+            for h in range(2):
+                arrived(block(rp, j, h), rp_sem.at[j, h])
+                arrived(block(rm, j, h), rm_sem.at[j, h])
+
+        def half(h, carry):
+            rows = pl.ds(pl.multiple_of(h * HALF, HALF), HALF)
+            acc = jnp.dot(a[p, rows, :], b[:, cols], preferred_element_type=jnp.float32)
+            if p == 0:
+                s0[rows, cols] = acc.astype(jnp.bfloat16)
+            elif p == 1:
+                s1[rows, cols] = (acc + rf[rows, cols].astype(jnp.float32)).astype(jnp.bfloat16)
+            elif p == 2:
+                s2[rows, cols] = acc.astype(jnp.bfloat16)
+            else:
+                out[rows, cols] = (
+                    acc + rp[rows, cols].astype(jnp.float32) + rm[rows, cols].astype(jnp.float32)
+                )
+            return carry
+
+        lax.fori_loop(0, 2, half, 0)
+        if p == 0:
+            push(block(s0, j, 0), block(rf, j, 0), x_snd.at[p, j, 0], rf_sem.at[j, 0], xr)
+            push(block(s0, j, 1), block(rf, j, 1), x_snd.at[p, j, 1], rf_sem.at[j, 1], xl)
+        elif p == 1:
+            push(block(s1, j, 0), block(rp, j, 0), x_snd.at[p, j, 0], rp_sem.at[j, 0], xr)
+            push(block(s1, j, 1), block(rm, j, 1), x_snd.at[p, j, 1], rm_sem.at[j, 1], xl)
+        elif p == 2:
+            push(block(s2, j, 0), block(rm, j, 0), x_snd.at[p, j, 0], rm_sem.at[j, 0], xl)
+            push(block(s2, j, 1), block(rp, j, 1), x_snd.at[p, j, 1], rp_sem.at[j, 1], xr)
+        else:
+            copy = pltpu.make_async_copy(out.at[:, cols], o_ref.at[:, cols], o_sem.at[j])
+            copy.start()
+            finals.append(copy)
+
+    finals = []
+    for r in (2, 1, 3, 0):
+        a2(r)
+    steps = {
+        "a_own": a_own, "a_relay": a_relay, "a_fwd": a_fwd, "a_far": a_far, "a_done": a_done,
+        "b_own": b_own, "b_relay": b_relay, "b_done": b_done, "unit": unit,
+    }
+    own_copy.start()
+    for name, *rest in plan()[0]:
+        steps[name](*rest)
+    for cond, copy in pending:
+        if cond is None:
+            copy.wait_send()
+        else:
+            pl.when(cond)(copy.wait_send)
+    for copy in finals:
+        copy.wait()
+
+
+def square(tile):
+    dma = pltpu.SemaphoreType.DMA
+    bf = jnp.bfloat16
+    return pl.pallas_call(
+        square_kernel,
+        out_shape=jax.ShapeDtypeStruct((ROWS, COLS), jnp.float32),
+        in_specs=[pl.BlockSpec(memory_space=pltpu.VMEM)],
+        out_specs=pl.BlockSpec(memory_space=pl.ANY),
+        scratch_shapes=[
+            pltpu.VMEM((4, ROWS, K), bf),
+            pltpu.VMEM((K, COLS), bf),
+            pltpu.VMEM((ROWS, COLS), bf),
+            pltpu.VMEM((ROWS, COLS), bf),
+            pltpu.VMEM((ROWS, COLS), bf),
+            pltpu.VMEM((ROWS, COLS), bf),
+            pltpu.VMEM((ROWS, COLS), bf),
+            pltpu.VMEM((ROWS, COLS), bf),
+            pltpu.VMEM((ROWS, COLS), jnp.float32),
+            dma((4, 2)), dma((4, 2)), dma((4, 2)), dma((4, 2)), dma((4, 4)),
+            dma((NJ, 2)), dma((NJ, 2)), dma((NJ, 2)), dma((NJ, 2)), dma((NJ, 2)), dma((NJ, 2)),
+            dma((4, 2, 2)), dma((1,)), dma((4, 6)), dma((4, 4)), dma((NJ, 6)), dma((3, NJ, 2)),
+            dma((2,)), dma((NJ,)),
+        ],
+        compiler_params=pltpu.CompilerParams(
+            collective_id=0, has_side_effects=True, vmem_limit_bytes=60 * 2**20
+        ),
+        name="square",
+    )(tile)
 
 
 def features(edge_vec):
@@ -88,12 +390,7 @@
     diagonal_mask = global_rows[:, None] == global_cols[None, :]
     shifted = jnp.where(diagonal_mask, upper_bound[0], jnp.float32(0.0)) - hamiltonian
     start_density = (shifted / (upper_bound[0] - lower_bound[0])).astype(jnp.bfloat16)
-    row_strip = lax.all_gather(start_density, "col", axis=1, tiled=True)
-    return jnp.dot(
-        row_strip,
-        lax.all_gather(start_density, "row", axis=0, tiled=True),
-        preferred_element_type=jnp.float32,
-    )
+    return square(start_density)
 
 
 def solution(mesh):

time: 438 us -> 221 us (0.50)
  waiting for transfers between devices: 313 us -> 0 us
  Pallas kernels: 0 us -> 141 us
  matrix products: 41.4 us -> 7.53 us
  between operations: 14.8 us -> 1.48 us
    all_gather x2 -> x0, waiting for transfers between devices: 312 us -> none  [the longest x1 221 us: shards(): lax.all_gather(start_density, 'row', axis=0, tiled=True)]
    pallas_call x0 -> x1, Pallas kernels: none -> 141 us  [square(): pl.pallas_call(square_kernel, out_shape=jax.ShapeDtypeStruct((ROWS, COLS)...]
    dot_general x1 -> x0, matrix products: 36.2 us -> none  [shards(): jnp.dot(row_strip, lax.all_gather(start_density, 'row', axis=0, tiled=Tru...]
    unnamed x9 -> x10, local copies, waits for them, and re-layouts: 6.82 us -> 9.43 us
  transfers between devices with their start and end apart: 2 -> 0, of which waited for: 2 -> 0; matrix products, arithmetic and copies ran while one was open for 0% -> 0% of each run, Pallas kernels for 0% -> 0%
where the time goes in v1:
time: 221 us
  Pallas kernels  141 us (64%)
  blocking collectives  39.6 us (18%)
  local copies, waits for them, and re-layouts  16.8 us (8%)
  other arithmetic  14.5 us (7%)
  matrix products  7.53 us (3%)
    pallas_call x1, Pallas kernels, square(): pl.pallas_call(square_kernel, out_shape=jax.ShapeDtypeStruct((ROWS, COLS)...  141 us
    all_gather x1, blocking collectives, shards(): gathered = lax.all_gather(packed, ('row', 'col'), axis=1, tiled=True)  39.6 us
    unnamed x10, local copies, waits for them, and re-layouts  9.43 us
    reshape x1, local copies, waits for them, and re-layouts, shards(): blocks_back = jnp.dot(coefficient_back, block_weight, preferred_element_t...  6.6 us
    convert_element_type x1, other arithmetic, shards(): (shifted / (upper_bound[0] - lower_bound[0])).astype(jnp.bfloat16)  5.86 us
    add x1, other arithmetic, shards(): blocks + blocks_back.transpose(0, 1, 3, 2)  5.62 us

profile of v1, /device:TPU:1, one launch (start us, length us, event | category | flops | bytes accessed | tf_op | source)
XLA Modules:
  0.0 220.9 jit_solution(4032772116205177804)
XLA Ops:
  0.0 0.7 multiply_reduce_fusion
  0.7 0.8 multiply_subtract_fusion
  1.5 0.8 fusion.6
  2.3 0.1 copy.13
  2.5 0.1 broadcast_multiply_fusion
  2.6 0.1 mul.81
  2.7 0.8 copy.14
  3.6 39.6 %all_gather.3 = f32[146,1024]{0,1:T(8,128)S(1)} all-gather(f32[146,8]{0,1:T(8,128)S(1)} %pad_maximum_fusion), channel_id=1, replica_groups=mesh['row'=16,'col'=8] {'row','col'}, dimensions={1}, use_global_device_ids=true | all-gather | bytes 602688 | tf_op jit(solution)/shard_map/all_gather | solution.py:340
  43.2 0.2 slice_convert_fusion
  43.4 0.5 slice_reduce_fusion.1
  43.9 0.1 broadcast_compare_fusion.1
  44.0 0.1 broadcast_compare_fusion.3
  44.1 0.1 broadcast_and_fusion
  44.3 0.5 convolution_convert_fusion
  44.8 3.1 %convolution_bitcast_fusion = f32[9,8,128,128]{3,1,2,0:T(8,128)S(1)} fusion(bf16[72,144]{1,0:T(8,128)(2,1)S(1)} %convolution_convert_fusion, bf16[144,16384]{1,0:T(8,128)(2,1)} %param.8), kind=kOutput, calls=%fused_computation.5 | convolution fusion | flops 339738624 | bytes 9457920 | tf_op jit(solution)/shard_map/dot_general | solution.py:377
  47.9 3.0 %copy.18 = f32[9,8,128,128]{3,2,1,0:T(8,128)} copy(f32[9,8,128,128]{3,1,2,0:T(8,128)S(1)} %convolution_bitcast_fusion) | data formatting | bytes 9437184
  50.9 6.6 %copy.15 = f32[6,12,128,128]{2,1,3,0:T(8,128)} copy(f32[6,12,128,128]{3,2,1,0:T(8,128)} %bitcast.50) | data formatting | bytes 9437184 | tf_op jit(solution)/shard_map/reshape | solution.py:379
  57.6 0.5 convolution_convert_fusion.1
  58.1 3.4 %convolution_bitcast_fusion.1 = f32[9,8,128,128]{3,1,2,0:T(8,128)S(1)} fusion(bf16[72,144]{1,0:T(8,128)(2,1)S(1)} %convolution_convert_fusion.1, bf16[144,16384]{1,0:T(8,128)(2,1)} %param.8), kind=kOutput, calls=%fused_computation.6 | convolution fusion | flops 339738624 | bytes 9457920 | tf_op jit(solution)/shard_map/dot_general | solution.py:374
  61.5 0.8 copy.17
  62.4 5.6 %bitcast_add_fusion = f32[6,12,128,128]{3,1,2,0:T(8,128)} fusion(f32[6,12,128,128]{2,1,3,0:T(8,128)S(1)} %bitcast.48, f32[6,12,128,128]{3,2,1,0:T(8,128)S(1)} %bitcast.49), kind=kLoop, calls=%fused_computation | loop fusion | flops 1179648 | bytes 14155776 | tf_op jit(solution)/shard_map/add | solution.py:383
  69.3 5.9 %fusion.2.t_ref = bf16[768,1536]{1,0:T(8,128)(2,1)} fusion(f32[96,8,12,128]{3,2,1,0:T(8,128)} %bitcast.46, bf16[768,1536]{1,0:T(8,128)(2,1)S(1)} %copy-done, f32[]{:T(128)S(6)} %sub.36, f32[]{:T(128)} %bitcast.44, s32[1536]{0:T(1024)S(1)} %iota_add_fusion, s32[768]{0:T(1024)S(1)} %iota_add_fusion.1), kind=kLoop, calls=%fused_computation.4 | loop fusion | flops 8257536 | bytes 9446408 | tf_op jit(solution)/shard_map/convert_element_type | solution.py:392
  75.2 140.9 %square.10 = f32[768,1536]{1,0:T(8,128)} custom-call(bf16[768,1536]{1,0:T(8,128)(2,1)} %fusion.2.t_ref), custom_call_target="tpu_custom_call" | custom-call | tf_op jit(solution)/shard_map/square/pallas_call | solution.py:286
  216.0 4.8 %copy.25 = f32[768,1536]{1,0:T(8,128)} copy(f32[768,1536]{1,0:T(8,128)} %square.10) | data formatting | bytes 9437184
  (21 shorter events, 0.3 us)
Async XLA Ops:
  57.6 4.7 %slice-start = ((s8[6291456]{0:T(1024)(128)(4,1)}), s8[4194304]{0:T(1024)(128)(4,1)S(1)}, s32[]{:S(2)}) async-start(s8[6291456]{0:T(1024)(128)(4,1)} %bitcast.47), calls=%async_computation | async-start | bytes 8388608
  58.1 4.2 %slice-start.1 = ((s8[6291456]{0:T(1024)(128)(4,1)}), s8[2097152]{0:T(1024)(128)(4,1)S(1)}, s32[]{:S(2)}) async-start(s8[6291456]{0:T(1024)(128)(4,1)} %bitcast.47), calls=%async_computation.1 | async-start | bytes 4194304
  62.4 6.9 %copy-start = (bf16[768,1536]{1,0:T(8,128)(2,1)S(1)}, bf16[768,1536]{1,0:T(8,128)(2,1)}, u32[]{:S(2)}) copy-start(bf16[768,1536]{1,0:T(8,128)(2,1)} %param.9) | copy-start | bytes 7077892

commit v2 on v1

--- a/solution.py
+++ b/solution.py
@@ -8,6 +8,11 @@
 ORB = 128
 NR = 16
 RB = 6
+CB = 12
+NB = 96
+FEAT = 144
+EDGES = 1024
+PAIRS = RB * CB
 ROWS = 768
 COLS = 1536
 K = 3072
@@ -310,87 +315,177 @@
     )(tile)
 
 
-def features(edge_vec):
-    squared = jnp.sum(edge_vec * edge_vec, axis=0)
-    radius = jnp.sqrt(squared + 0.25)
-    unit_x = edge_vec[0] / radius
-    unit_y = edge_vec[1] / radius
-    unit_z = edge_vec[2] / radius
-    harmonics = jnp.stack(
-        [
-            jnp.ones_like(unit_x),
-            unit_x,
-            unit_y,
-            unit_z,
-            unit_x * unit_y,
-            unit_y * unit_z,
-            unit_z * unit_x,
-            unit_x * unit_x - unit_y * unit_y,
-            3.0 * unit_z * unit_z - 1.0,
-        ]
+def density_kernel(
+    edge_ref, lower_ref, upper_ref, w_hbm, base_hbm, t_ref,
+    edges, emb, wide, sel, w, base, direct, mirror,
+    w_sem, base_sem, own_sem, snd, rcv,
+):
+    row = lax.axis_index("row")
+    col = lax.axis_index("col")
+    w_copy = pltpu.make_async_copy(w_hbm, w, w_sem)
+    base_copy = pltpu.make_async_copy(base_hbm, base, base_sem)
+    w_copy.start()
+    base_copy.start()
+
+    barrier = pltpu.get_barrier_semaphore()
+    for d in range(1, 8):
+        pl.semaphore_signal(
+            barrier, inc=1, device_id=(row, (col + d) % 8), device_id_type=MESH
+        )
+    for d in range(1, 16):
+        pl.semaphore_signal(
+            barrier, inc=1, device_id=((row + d) % 16, col), device_id_type=MESH
+        )
+    pl.semaphore_wait(barrier, 22)
+
+    mine = row * 8 + col
+    own = pltpu.make_async_copy(edge_ref, edges.at[pl.ds(mine, 1), :], own_sem)
+    own.start()
+    copies = []
+    for d in range(1, 8):
+        copy = pltpu.make_async_remote_copy(
+            src_ref=edge_ref, dst_ref=edges.at[pl.ds(mine, 1), :],
+            send_sem=snd.at[d], recv_sem=rcv.at[d],
+            device_id=(row, (col + d) % 8), device_id_type=MESH,
+        )
+        copy.start()
+        copies.append(copy)
+    own.wait()
+    for d in range(1, 8):
+        src = row * 8 + (col + 8 - d) % 8
+        pltpu.make_async_remote_copy(
+            src_ref=edge_ref, dst_ref=edges.at[pl.ds(src, 1), :],
+            send_sem=snd.at[d], recv_sem=rcv.at[d],
+            device_id=(row, (col + d) % 8), device_id_type=MESH,
+        ).wait_recv()
+
+    def group(r):
+        return edges.at[pl.ds(pl.multiple_of(r * 8, 8), 8), :]
+
+    for d in range(1, 16):
+        copy = pltpu.make_async_remote_copy(
+            src_ref=group(row), dst_ref=group(row),
+            send_sem=snd.at[7 + d], recv_sem=rcv.at[7 + d],
+            device_id=((row + d) % 16, col), device_id_type=MESH,
+        )
+        copy.start()
+        copies.append(copy)
+    for d in range(1, 16):
+        src = (row + 16 - d) % 16
+        pltpu.make_async_remote_copy(
+            src_ref=group(src), dst_ref=group(src),
+            send_sem=snd.at[7 + d], recv_sem=rcv.at[7 + d],
+            device_id=((row + d) % 16, col), device_id_type=MESH,
+        ).wait_recv()
+    for copy in copies:
+        copy.wait_send()
+
+    fields = edges[...].T
+    vx, vy, vz = fields[0:8], fields[8:16], fields[16:24]
+    first, second = fields[24:32], fields[32:40]
+    radius = jnp.sqrt(vx * vx + vy * vy + vz * vz + 0.25)
+    ux, uy, uz = vx / radius, vy / radius, vz / radius
+    harmonics = [
+        None, ux, uy, uz, ux * uy, uy * uz, uz * ux, ux * ux - uy * uy, 3.0 * uz * uz - 1.0
+    ]
+    for k in range(NR):
+        scaled = (radius - (1.0 + 0.3 * k)) / 0.5
+        radial = jnp.exp(-(scaled * scaled))
+        for m in range(9):
+            f = 9 * k + m
+            emb[f * 8 : f * 8 + 8, :] = radial if m == 0 else radial * harmonics[m]
+    number = lax.broadcasted_iota(jnp.int32, (PAIRS, ORB), 0)
+    upper_atom = jnp.zeros((PAIRS, ORB), jnp.int32)
+    for n in range(1, RB):
+        upper_atom = upper_atom + jnp.where(number >= CB * n, 1, 0)
+    pair = (row * RB + upper_atom) * NB + col * CB + number - CB * upper_atom
+    pair = pair.astype(jnp.float32)
+    forward = first * float(NB) + second
+    backward = second * float(NB) + first
+    for i in range(8):
+        lanes = slice(i * ORB, (i + 1) * ORB)
+        sel[0:PAIRS, lanes] = jnp.where(forward[i : i + 1] == pair, 1.0, 0.0)
+        sel[PAIRS : 2 * PAIRS, lanes] = jnp.where(backward[i : i + 1] == pair, 1.0, 0.0)
+        wide[:, lanes] = emb[pl.ds(i, FEAT, stride=8), :]
+    coefficient = lax.dot_general(
+        sel[...], wide[...], (((1,), (1,)), ((), ())),
+        precision=lax.Precision.HIGHEST, preferred_element_type=jnp.float32,
+    ).astype(jnp.bfloat16)
+
+    w_copy.wait()
+
+    def expand(n, carry):
+        start = pl.multiple_of(n * 8 * ORB, 8 * ORB)
+        part = jnp.dot(
+            coefficient, w[:, pl.ds(start, 8 * ORB)], preferred_element_type=jnp.float32
+        )
+        for s in range(8):
+            for g in range(PAIRS // 8):
+                place = pl.ds(g * 8 * ORB + n * 8 + s, 8, stride=ORB)
+                lanes = slice(s * ORB, (s + 1) * ORB)
+                direct[place, :] = part[g * 8 : g * 8 + 8, lanes]
+                mirror[place, :] = part[PAIRS + g * 8 : PAIRS + g * 8 + 8, lanes]
+        return carry
+
+    lax.fori_loop(0, ORB // 8, expand, 0)
+    base_copy.wait()
+    upper = upper_ref[0]
+    scale = upper - lower_ref[0]
+    on_diagonal = lax.broadcasted_iota(jnp.int32, (ORB, ORB), 0) == lax.broadcasted_iota(
+        jnp.int32, (ORB, ORB), 1
     )
-    centers = 1.0 + 0.3 * jnp.arange(NR, dtype=jnp.float32)
-    radial = jnp.exp(-jnp.square((radius[None, :] - centers[:, None]) / 0.5))
-    return (radial[:, None, :] * harmonics[None, :, :]).reshape(NR * 9, edge_vec.shape[1])
+    for i in range(RB):
+
+        def finish(k, carry):
+            at = pl.multiple_of((i * CB + k) * ORB, ORB)
+            lanes = pl.ds(pl.multiple_of(k * ORB, ORB), ORB)
+            rows = slice(i * ORB, (i + 1) * ORB)
+            both = direct[pl.ds(at, ORB), :] + mirror[pl.ds(at, ORB), :].T
+            both = both + base[rows, lanes].astype(jnp.float32)
+            shift = jnp.where(row * RB + i == col * CB + k, upper, 0.0)
+            moved = jnp.where(on_diagonal, shift, 0.0) - both
+            t_ref[rows, lanes] = (moved / scale).astype(jnp.bfloat16)
+            return carry
+
+        lax.fori_loop(0, CB, finish, 0)
+
+
+def density(edges, lower, upper, weight, base):
+    dma = pltpu.SemaphoreType.DMA
+    f32 = jnp.float32
+    return pl.pallas_call(
+        density_kernel,
+        out_shape=jax.ShapeDtypeStruct((ROWS, COLS), jnp.bfloat16),
+        in_specs=[
+            pl.BlockSpec(memory_space=pltpu.VMEM),
+            pl.BlockSpec(memory_space=pltpu.SMEM),
+            pl.BlockSpec(memory_space=pltpu.SMEM),
+            pl.BlockSpec(memory_space=pl.ANY),
+            pl.BlockSpec(memory_space=pl.ANY),
+        ],
+        out_specs=pl.BlockSpec(memory_space=pltpu.VMEM),
+        scratch_shapes=[
+            pltpu.VMEM((ORB, ORB), f32),
+            pltpu.VMEM((FEAT * 8, ORB), f32),
+            pltpu.VMEM((FEAT, EDGES), f32),
+            pltpu.VMEM((2 * PAIRS, EDGES), f32),
+            pltpu.VMEM((FEAT, ORB * ORB), jnp.bfloat16),
+            pltpu.VMEM((ROWS, COLS), jnp.bfloat16),
+            pltpu.VMEM((PAIRS * ORB, ORB), f32),
+            pltpu.VMEM((PAIRS * ORB, ORB), f32),
+            dma, dma, dma, dma((23,)), dma((23,)),
+        ],
+        compiler_params=pltpu.CompilerParams(
+            collective_id=1, has_side_effects=True, vmem_limit_bytes=60 * 2**20
+        ),
+        name="density",
+    )(edges, lower, upper, weight, base)
 
 
 def shards(edge_vec, edge_atoms, block_weight, base_hamiltonian, lower_bound, upper_bound):
-    atoms_float = edge_atoms.astype(jnp.float32)
-    packed = jnp.concatenate([features(edge_vec), atoms_float], axis=0)
-    gathered = lax.all_gather(packed, ("row", "col"), axis=1, tiled=True)
-    embedding = gathered[:-2]
-    atom_pairs = gathered[-2:].astype(jnp.int32)
-    first_atom = atom_pairs[0]
-    second_atom = atom_pairs[1]
-    atoms_total = RB * lax.axis_size("row")
-    col_blocks = atoms_total // lax.axis_size("col")
-    row_index = lax.axis_index("row")
-    col_index = lax.axis_index("col")
-    row_atoms = row_index * RB + jnp.arange(RB, dtype=jnp.int32)
-    col_atoms = col_index * col_blocks + jnp.arange(col_blocks, dtype=jnp.int32)
-    direct = (
-        (
-            (first_atom[None, None, :] == row_atoms[:, None, None])
-            & (second_atom[None, None, :] == col_atoms[None, :, None])
-        )
-        .astype(jnp.float32)
-        .reshape(RB * col_blocks, -1)
-    )
-    mirror = (
-        (
-            (first_atom[None, None, :] == col_atoms[None, :, None])
-            & (second_atom[None, None, :] == row_atoms[:, None, None])
-        )
-        .astype(jnp.float32)
-        .reshape(RB * col_blocks, -1)
-    )
-    contract = (((1,), (1,)), ((), ()))
-    coefficient = lax.dot_general(
-        direct, embedding, contract, precision=lax.Precision.HIGHEST
-    ).astype(jnp.bfloat16)
-    coefficient_back = lax.dot_general(
-        mirror, embedding, contract, precision=lax.Precision.HIGHEST
-    ).astype(jnp.bfloat16)
-    blocks = jnp.dot(coefficient, block_weight, preferred_element_type=jnp.float32).reshape(
-        RB, col_blocks, ORB, ORB
-    )
-    blocks_back = jnp.dot(
-        coefficient_back, block_weight, preferred_element_type=jnp.float32
-    ).reshape(RB, col_blocks, ORB, ORB)
-    tile_rows = RB * ORB
-    tile_cols = col_blocks * ORB
-    hamiltonian = (
-        (blocks + blocks_back.transpose(0, 1, 3, 2))
-        .transpose(0, 2, 1, 3)
-        .reshape(tile_rows, tile_cols)
-    )
-    hamiltonian = hamiltonian + base_hamiltonian.astype(jnp.float32)
-    global_rows = row_index * tile_rows + jnp.arange(tile_rows, dtype=jnp.int32)
-    global_cols = col_index * tile_cols + jnp.arange(tile_cols, dtype=jnp.int32)
-    diagonal_mask = global_rows[:, None] == global_cols[None, :]
-    shifted = jnp.where(diagonal_mask, upper_bound[0], jnp.float32(0.0)) - hamiltonian
-    start_density = (shifted / (upper_bound[0] - lower_bound[0])).astype(jnp.bfloat16)
-    return square(start_density)
+    packed = jnp.concatenate([edge_vec, edge_atoms.astype(jnp.float32)], axis=0)
+    packed = jnp.pad(packed.reshape(1, 40), ((0, 0), (0, ORB - 40)))
+    return square(density(packed, lower_bound, upper_bound, block_weight, base_hamiltonian))
 
 
 def solution(mesh):

time: 221 us -> 185 us (0.84)
  blocking collectives: 39.6 us -> 0 us
  Pallas kernels: 141 us -> 177 us
  other arithmetic: 14.5 us -> 1.37 us
  local copies, waits for them, and re-layouts: 16.8 us -> 5.44 us
  matrix products: 7.53 us -> 0 us
    all_gather x1 -> x0, blocking collectives: 39.6 us -> none  [shards(): gathered = lax.all_gather(packed, ('row', 'col'), axis=1, tiled=True)]
    pallas_call x0 -> x1, Pallas kernels: none -> 34.3 us  [density(): pl.pallas_call(density_kernel, out_shape=jax.ShapeDtypeStruct((ROWS, COLS...]
    dot_general x4 -> x0, matrix products: 7.53 us -> none  [the longest x1 3.38 us: shards(): jnp.dot(coefficient, block_weight, preferred_element_type=jnp.float32)]
    reshape x1, local copies, waits for them, and re-layouts: 6.6 us -> 0.08 us  [shards(): packed = jnp.pad(packed.reshape(1, 40), ((0, 0), (0, ORB - 40)))]
    add x6 -> x0, other arithmetic: 5.64 us -> none  [the longest x1 5.62 us: shards(): blocks + blocks_back.transpose(0, 1, 3, 2)]
    convert_element_type x3 -> x1, other arithmetic: 6.07 us -> 0.68 us  [shards(): packed = jnp.concatenate([edge_vec, edge_atoms.astype(jnp.float32)], axis=0)]
    unnamed x10 -> x1, local copies, waits for them, and re-layouts: 9.43 us -> 4.84 us
where the time goes in v2:
time: 185 us
  Pallas kernels  177 us (96%)
  local copies, waits for them, and re-layouts  5.44 us (3%)
    pallas_call x1, Pallas kernels, square(): pl.pallas_call(square_kernel, out_shape=jax.ShapeDtypeStruct((ROWS, COLS)...  142 us
    pallas_call x1, Pallas kernels, density(): pl.pallas_call(density_kernel, out_shape=jax.ShapeDtypeStruct((ROWS, COLS...  34.3 us
    unnamed x1, local copies, waits for them, and re-layouts  4.84 us

profile of v2, /device:TPU:1, one launch (start us, length us, event | category | flops | bytes accessed | tf_op | source)
XLA Modules:
  0.0 184.8 jit_solution(16670582651799711453)
XLA Ops:
  1.3 0.7 convert_element_type.5
  2.0 0.7 pad_maximum_fusion
  2.7 0.1 reshape.3
  2.8 0.5 pad.4.edge_ref
  3.3 34.3 %density.1.t_ref = bf16[768,1536]{1,0:T(8,128)(2,1)} custom-call(f32[1,128]{1,0:T(1,128)} %pad.4.edge_ref, f32[1]{0:T(128)S(6)} %copy.8.lower_ref, f32[1]{0:T(128)S(6)} %copy.9.upper_ref, bf16[144,16384]{1,0:T(8,128)(2,1)} %w_hbm.1, bf16[768,1536]{1,0:T(8,128)(2,1)} %base_hbm.1), custom_call_target="tpu_custom_call" | custom-call | tf_op jit(solution)/shard_map/density/pallas_call | solution.py:456
  37.6 142.4 %square.1 = f32[768,1536]{1,0:T(8,128)} custom-call(bf16[768,1536]{1,0:T(8,128)(2,1)} %density.1.t_ref), custom_call_target="tpu_custom_call" | custom-call | tf_op jit(solution)/shard_map/square/pallas_call | solution.py:291
  180.0 4.8 %copy.10 = f32[768,1536]{1,0:T(8,128)} copy(f32[768,1536]{1,0:T(8,128)} %square.1) | data formatting | bytes 9437184

commit v3 on v2

--- a/solution.py
+++ b/solution.py
@@ -20,36 +20,40 @@
 JW = COLS // NJ
 HALF = ROWS // 2
 QUART = ROWS // 4
+SUB = ROWS // 8
 MESH = pl.DeviceIdType.MESH
 
 
 def plan():
-    z_period, y_period, y_lead = 12.7, 19.0, 8.0
-    unit_us, out_us, lag = 1.6, 4.3, 2.0
-    events = []
+    z_period, y_period = 12.7, 9.5
+    unit_us, out_us, lag = 0.85, 2.15, 2.5
+    ring = [4, 5, 0, 1, 2, 3, 7]
+    events = [(0.0, "a_own", 6), (0.0, "b_own", 0), (6.0, "a_own", ring[0])]
     for j in range(NJ):
-        if j == 0:
-            events.append((0.0, "b_own", j))
         events.append((z_period * j + 5.7, "b_relay", j))
         if j + 1 < NJ:
             events.append((z_period * j + 5.8, "b_own", j + 1))
-        events.append((z_period * (j + 1) + 2.0, "b_done", j))
-    for p in range(4):
-        start = y_lead + y_period * p
-        if p == 0:
-            events.append((start, "a_own", p))
-        events.append((start + 8.0, "a_relay", p))
-        if p + 1 < 4:
-            events.append((start + 8.1, "a_own", p + 1))
-        events.append((start + 14.5, "a_fwd", p))
-        events.append((start + y_period + 1.5, "a_far", p))
-        events.append((start + y_period + 4.0, "a_done", p))
+        events.append((z_period * (j + 1) + 2.5, "b_done", j))
+    events.append((17.0, "a_fwd", 6))
+    for i, p in enumerate(ring):
+        start = 6.3 + y_period * i
+        events.append((start + 5.0, "a_relay", p))
+        if i + 1 < len(ring):
+            events.append((start + 5.1, "a_own", ring[i + 1]))
+        else:
+            events.append((start + 5.1, "a_relay", 6))
+        events.append((start + 8.3, "a_fwd", p))
+        events.append((start + y_period + 2.0, "a_far", p))
+        events.append((start + y_period + 4.5, "a_done", p))
+    last = 6.3 + y_period * len(ring)
+    events.append((last + 5.0, "a_far", 6))
+    events.append((last + 7.5, "a_done", 6))
     events.sort(key=lambda e: e[0])
     order = []
     now, link = 0.0, 0.0
     a_ok, b_ok = set(), set()
     arrive = {}
-    todo = [(p, j) for j in range(NJ) for p in (0, 2, 1, 3)]
+    todo = [(p, j) for j in range(NJ) for p in range(8)]
     while todo or events:
         while events and events[0][0] <= now:
             _, name, arg = events.pop(0)
@@ -63,12 +67,13 @@
         for p, j in todo:
             if p not in a_ok or j not in b_ok:
                 continue
-            needs = {0: [], 1: [(0, j)], 2: [], 3: [(1, j), (2, j)]}[p]
+            kind, q = p // 2, p % 2
+            needs = {0: [], 1: [(q, j)], 2: [], 3: [(2 + q, j), (4 + q, j)]}[kind]
             if any(n not in arrive for n in needs):
                 continue
             at = max([now] + [arrive[n] for n in needs])
             if at <= now:
-                rank = (p == 3, j, {0: 0, 2: 1, 1: 2, 3: 3}[p])
+                rank = (kind == 3, kind == 1, j, p)
                 if best is None or rank < best[0]:
                     best = (rank, (p, j))
             else:
@@ -80,7 +85,7 @@
         todo.remove((p, j))
         order.append(("unit", p, j))
         now += unit_us
-        if p != 3:
+        if p < 6:
             link = max(link, now) + out_us
             arrive[(p, j)] = link + lag
     return order, now
@@ -89,7 +94,7 @@
 def square_kernel(
     t_ref, o_ref, a, b, s0, s1, s2, rf, rp, rm, out,
     a2_sem, al_sem, ar_sem, af_sem, sb_sem, bl_sem, br_sem, bf_sem, rf_sem, rp_sem, rm_sem,
-    a2_snd, a_snd, ay_snd, sb_snd, b_snd, x_snd, own_sem, o_sem,
+    a2_snd, ay_snd, sb_snd, b_snd, x_snd, own_sem, o_sem,
 ):
     row = lax.axis_index("row")
     col = lax.axis_index("col")
@@ -125,72 +130,85 @@
     def arrived(dst, rcv):
         remote(dst, dst, own_sem.at[1], rcv, sib).wait_recv()
 
-    def a2(r):
+    def exchange(r, h, q):
         kk = mod(x - r)
         active = (kk // 2) == c
         cols = pl.ds(pl.multiple_of((kk % 2) * ROWS, ROWS), ROWS)
         place = pl.ds(pl.multiple_of(y * ROWS, ROWS), ROWS)
+        p = 2 * {0: 3, 2: 0, 1: 1 + h, 3: 2 - h}[r] + q
         for s in range(2):
-            for h in range(2):
-                p = {0: 3, 2: 0, 1: 1 + h, 3: 2 - h}[r]
-                rows = pl.ds(h * HALF + s * QUART, QUART)
-                src = t_ref.at[rows, cols]
-                dst = a.at[p, rows, place]
-                if r:
-                    copy = remote(src, dst, a2_snd.at[r, s, h], a2_sem.at[p, s], dev(z, kk, y, h))
-                    cond = active
-                    pl.when(cond)(copy.start)
-                    pending.append((cond, copy))
-                else:
-                    copy = remote(src, dst, a2_snd.at[r, s, h], a2_sem.at[p, s], sib)
-                    cond = active & (c != h)
-                    pl.when(cond)(copy.start)
-                    pending.append((cond, copy))
-                    local = pltpu.make_async_copy(src, dst, a2_sem.at[p, s])
-                    pl.when(active & (c == h))(local.start)
+            src = t_ref.at[pl.ds(h * HALF + q * QUART + s * SUB, SUB), cols]
+            dst = a.at[p, pl.ds(h * QUART + s * SUB, SUB), place]
+            snd, rcv = a2_snd.at[r, h, q, s], a2_sem.at[p, s]
+            if r:
+                copy = remote(src, dst, snd, rcv, dev(z, kk, y, h))
+                pl.when(active)(copy.start)
+                pending.append((active, copy))
+            else:
+                copy = remote(src, dst, snd, rcv, sib)
+                cond = active & (c != h)
+                pl.when(cond)(copy.start)
+                pending.append((cond, copy))
+                local = pltpu.make_async_copy(src, dst, rcv)
+                pl.when(active & (c == h))(local.start)
 
     def a_piece(p, s, yy):
         return a.at[
             p,
-            pl.ds(pl.multiple_of(c * HALF + s * QUART, QUART), QUART),
+            pl.ds(pl.multiple_of(c * QUART + s * SUB, SUB), SUB),
             pl.ds(pl.multiple_of(yy * ROWS, ROWS), ROWS),
         ]
 
     def a_half(p, yy, cc):
         return a.at[
             p,
-            pl.ds(pl.multiple_of(cc * HALF, HALF), HALF),
+            pl.ds(pl.multiple_of(cc * QUART, QUART), QUART),
             pl.ds(pl.multiple_of(yy * ROWS, ROWS), ROWS),
         ]
 
+    def along(p, s, yy, snd, rcv, target):
+        push(a_piece(p, s, yy), a_piece(p, s, yy), ay_snd.at[p, snd], rcv.at[p, s], target)
+
+    def share(p, i, yy):
+        push(a_half(p, yy, c), a_half(p, yy, c), sb_snd.at[p, i], sb_sem.at[p, i], sib)
+
     def a_own(p):
         arrived(a_piece(p, 0, y), a2_sem.at[p, 0])
-        push(a_piece(p, 0, y), a_piece(p, 0, y), ay_snd.at[p, 0], al_sem.at[p, 0], yr)
+        along(p, 0, y, 0, al_sem, yr)
         arrived(a_piece(p, 1, y), a2_sem.at[p, 1])
-        push(a_piece(p, 1, y), a_piece(p, 1, y), ay_snd.at[p, 1], ar_sem.at[p, 1], yl)
-        push(a_piece(p, 1, y), a_piece(p, 1, y), ay_snd.at[p, 2], al_sem.at[p, 1], yr)
-        push(a_piece(p, 0, y), a_piece(p, 0, y), ay_snd.at[p, 3], ar_sem.at[p, 0], yl)
-        push(a_half(p, y, c), a_half(p, y, c), sb_snd.at[p, 0], sb_sem.at[p, 0], sib)
+        along(p, 1, y, 1, ar_sem, yl)
+        along(p, 1, y, 2, al_sem, yr)
+        along(p, 0, y, 3, ar_sem, yl)
+        share(p, 0, y)
 
     def a_relay(p):
         left, right = mod(y - 1), mod(y + 1)
         arrived(a_piece(p, 0, left), al_sem.at[p, 0])
-        push(a_piece(p, 0, left), a_piece(p, 0, left), ay_snd.at[p, 4], af_sem.at[p, 0], yr)
+        along(p, 0, left, 4, af_sem, yr)
         arrived(a_piece(p, 1, right), ar_sem.at[p, 1])
-        push(a_piece(p, 1, right), a_piece(p, 1, right), ay_snd.at[p, 5], af_sem.at[p, 1], yl)
+        along(p, 1, right, 5, af_sem, yl)
 
     def a_fwd(p):
         left, right = mod(y - 1), mod(y + 1)
         arrived(a_piece(p, 1, left), al_sem.at[p, 1])
-        push(a_half(p, left, c), a_half(p, left, c), sb_snd.at[p, 1], sb_sem.at[p, 1], sib)
+        if p == 6:
+            arrived(a_piece(p, 0, left), al_sem.at[p, 0])
+        share(p, 1, left)
         arrived(a_piece(p, 0, right), ar_sem.at[p, 0])
-        push(a_half(p, right, c), a_half(p, right, c), sb_snd.at[p, 2], sb_sem.at[p, 2], sib)
+        if p == 6:
+            arrived(a_piece(p, 1, right), ar_sem.at[p, 1])
+        share(p, 2, right)
+
+    def a_late(p):
+        left, right = mod(y - 1), mod(y + 1)
+        along(p, 0, left, 4, af_sem, yr)
+        along(p, 1, right, 5, af_sem, yl)
 
     def a_far(p):
         far = mod(y + 2)
         arrived(a_piece(p, 0, far), af_sem.at[p, 0])
         arrived(a_piece(p, 1, far), af_sem.at[p, 1])
-        push(a_half(p, far, c), a_half(p, far, c), sb_snd.at[p, 3], sb_sem.at[p, 3], sib)
+        share(p, 3, far)
 
     def a_done(p):
         for i, yy in enumerate((y, mod(y - 1), mod(y + 1), mod(y + 2))):
@@ -223,59 +241,62 @@
         for s in range(2):
             arrived(b_piece(j, s, mod(z + 2)), bf_sem.at[j, s])
 
-    def block(ref, j, h):
-        return ref.at[pl.ds(h * HALF, HALF), pl.ds(j * JW, JW)]
+    def block(ref, q, h, j):
+        return ref.at[pl.ds(q * HALF + h * QUART, QUART), pl.ds(j * JW, JW)]
 
     def unit(p, j):
+        kind, q = p // 2, p % 2
         cols = pl.ds(j * JW, JW)
-        if p == 1:
+        rows = pl.ds(q * HALF, HALF)
+        if kind == 1:
             for h in range(2):
-                arrived(block(rf, j, h), rf_sem.at[j, h])
-        if p == 3:
+                arrived(block(rf, q, h, j), rf_sem.at[q, h, j])
+        if kind == 3:
             for h in range(2):
-                arrived(block(rp, j, h), rp_sem.at[j, h])
-                arrived(block(rm, j, h), rm_sem.at[j, h])
-
-        def half(h, carry):
-            rows = pl.ds(pl.multiple_of(h * HALF, HALF), HALF)
-            acc = jnp.dot(a[p, rows, :], b[:, cols], preferred_element_type=jnp.float32)
-            if p == 0:
-                s0[rows, cols] = acc.astype(jnp.bfloat16)
-            elif p == 1:
-                s1[rows, cols] = (acc + rf[rows, cols].astype(jnp.float32)).astype(jnp.bfloat16)
-            elif p == 2:
-                s2[rows, cols] = acc.astype(jnp.bfloat16)
-            else:
-                out[rows, cols] = (
-                    acc + rp[rows, cols].astype(jnp.float32) + rm[rows, cols].astype(jnp.float32)
+                arrived(block(rp, q, h, j), rp_sem.at[q, h, j])
+                arrived(block(rm, q, h, j), rm_sem.at[q, h, j])
+        acc = jnp.dot(a[p], b[:, cols], preferred_element_type=jnp.float32)
+        if kind == 0:
+            s0[rows, cols] = acc.astype(jnp.bfloat16)
+        elif kind == 1:
+            s1[rows, cols] = (acc + rf[rows, cols].astype(jnp.float32)).astype(jnp.bfloat16)
+        elif kind == 2:
+            s2[rows, cols] = acc.astype(jnp.bfloat16)
+        else:
+            acc = acc + rp[rows, cols].astype(jnp.float32) + rm[rows, cols].astype(jnp.float32)
+            out[pl.ds(q * QUART, QUART), cols] = acc[:QUART]
+            out[pl.ds(HALF + q * QUART, QUART), cols] = acc[QUART:]
+        if kind == 3:
+            for h in range(2):
+                rows = pl.ds(h * HALF + q * QUART, QUART)
+                copy = pltpu.make_async_copy(out.at[rows, cols], o_ref.at[rows, cols], o_sem.at[q, h, j])
+                copy.start()
+                finals.append(copy)
+        else:
+            source = (s0, s1, s2)[kind]
+            for h in range(2):
+                target = xr if (h == 0) == (kind < 2) else xl
+                into, sem = (rf, rf_sem) if kind == 0 else (rp, rp_sem) if target is xr else (rm, rm_sem)
+                push(
+                    block(source, q, h, j), block(into, q, h, j),
+                    x_snd.at[p, h, j], sem.at[q, h, j], target,
                 )
-            return carry
-
-        lax.fori_loop(0, 2, half, 0)
-        if p == 0:
-            push(block(s0, j, 0), block(rf, j, 0), x_snd.at[p, j, 0], rf_sem.at[j, 0], xr)
-            push(block(s0, j, 1), block(rf, j, 1), x_snd.at[p, j, 1], rf_sem.at[j, 1], xl)
-        elif p == 1:
-            push(block(s1, j, 0), block(rp, j, 0), x_snd.at[p, j, 0], rp_sem.at[j, 0], xr)
-            push(block(s1, j, 1), block(rm, j, 1), x_snd.at[p, j, 1], rm_sem.at[j, 1], xl)
-        elif p == 2:
-            push(block(s2, j, 0), block(rm, j, 0), x_snd.at[p, j, 0], rm_sem.at[j, 0], xl)
-            push(block(s2, j, 1), block(rp, j, 1), x_snd.at[p, j, 1], rp_sem.at[j, 1], xr)
-        else:
-            copy = pltpu.make_async_copy(out.at[:, cols], o_ref.at[:, cols], o_sem.at[j])
-            copy.start()
-            finals.append(copy)
 
     finals = []
-    for r in (2, 1, 3, 0):
-        a2(r)
+    for r, hs in ((0, (0, 1)), (1, (1,)), (3, (0,)), (2, (0, 1)), (1, (0,)), (3, (1,))):
+        for q in range(2):
+            for h in hs:
+                exchange(r, h, q)
     steps = {
         "a_own": a_own, "a_relay": a_relay, "a_fwd": a_fwd, "a_far": a_far, "a_done": a_done,
         "b_own": b_own, "b_relay": b_relay, "b_done": b_done, "unit": unit,
     }
     own_copy.start()
     for name, *rest in plan()[0]:
-        steps[name](*rest)
+        if name == "a_relay" and rest == [6]:
+            a_late(6)
+        else:
+            steps[name](*rest)
     for cond, copy in pending:
         if cond is None:
             copy.wait_send()
@@ -294,7 +315,7 @@
         in_specs=[pl.BlockSpec(memory_space=pltpu.VMEM)],
         out_specs=pl.BlockSpec(memory_space=pl.ANY),
         scratch_shapes=[
-            pltpu.VMEM((4, ROWS, K), bf),
+            pltpu.VMEM((8, HALF, K), bf),
             pltpu.VMEM((K, COLS), bf),
             pltpu.VMEM((ROWS, COLS), bf),
             pltpu.VMEM((ROWS, COLS), bf),
@@ -303,10 +324,11 @@
             pltpu.VMEM((ROWS, COLS), bf),
             pltpu.VMEM((ROWS, COLS), bf),
             pltpu.VMEM((ROWS, COLS), jnp.float32),
-            dma((4, 2)), dma((4, 2)), dma((4, 2)), dma((4, 2)), dma((4, 4)),
-            dma((NJ, 2)), dma((NJ, 2)), dma((NJ, 2)), dma((NJ, 2)), dma((NJ, 2)), dma((NJ, 2)),
-            dma((4, 2, 2)), dma((1,)), dma((4, 6)), dma((4, 4)), dma((NJ, 6)), dma((3, NJ, 2)),
-            dma((2,)), dma((NJ,)),
+            dma((8, 2)), dma((8, 2)), dma((8, 2)), dma((8, 2)), dma((8, 4)),
+            dma((NJ, 2)), dma((NJ, 2)), dma((NJ, 2)),
+            dma((2, 2, NJ)), dma((2, 2, NJ)), dma((2, 2, NJ)),
+            dma((4, 2, 2, 2)), dma((8, 6)), dma((8, 4)), dma((NJ, 6)), dma((6, 2, NJ)),
+            dma((2,)), dma((2, 2, NJ)),
         ],
         compiler_params=pltpu.CompilerParams(
             collective_id=0, has_side_effects=True, vmem_limit_bytes=60 * 2**20

time: 185 us -> 169 us (0.914); the launches traced: 185 us -> 167 us
  Pallas kernels: 177 us -> 158 us
    pallas_call x1, Pallas kernels: 142 us -> 124 us  [square(): pl.pallas_call(square_kernel, out_shape=jax.ShapeDtypeStruct((ROWS, COLS)...]
where the time goes in v3:
time: 169 us; the launch traced here: 167 us
  Pallas kernels  158 us (93%)
  local copies, waits for them, and re-layouts  5.44 us (3%)
  between operations  1.76 us (1%)
    pallas_call x1, Pallas kernels, square(): pl.pallas_call(square_kernel, out_shape=jax.ShapeDtypeStruct((ROWS, COLS)...  124 us
    pallas_call x1, Pallas kernels, density(): pl.pallas_call(density_kernel, out_shape=jax.ShapeDtypeStruct((ROWS, COLS...  34.3 us
    unnamed x1, local copies, waits for them, and re-layouts  4.84 us

profile of v3, /device:TPU:1, one launch (start us, length us, event | category | flops | bytes accessed | tf_op | source)
XLA Modules:
  0.0 166.7 jit_solution(7516676495505840504)
XLA Ops:
  1.3 0.7 convert_element_type.5
  2.0 0.7 pad_maximum_fusion
  2.7 0.1 reshape.3
  2.8 0.5 pad.4.edge_ref
  3.3 34.3 %density.1.t_ref = bf16[768,1536]{1,0:T(8,128)(2,1)} custom-call(f32[1,128]{1,0:T(1,128)} %pad.4.edge_ref, f32[1]{0:T(128)S(6)} %copy.8.lower_ref, f32[1]{0:T(128)S(6)} %copy.9.upper_ref, bf16[144,16384]{1,0:T(8,128)(2,1)} %w_hbm.1, bf16[768,1536]{1,0:T(8,128)(2,1)} %base_hbm.1), custom_call_target="tpu_custom_call" | custom-call | tf_op jit(solution)/shard_map/density/pallas_call | solution.py:478
  37.6 123.9 %square.1 = f32[768,1536]{1,0:T(8,128)} custom-call(bf16[768,1536]{1,0:T(8,128)(2,1)} %density.1.t_ref), custom_call_target="tpu_custom_call" | custom-call | tf_op jit(solution)/shard_map/square/pallas_call | solution.py:312
  161.4 4.8 %copy.10 = f32[768,1536]{1,0:T(8,128)} copy(f32[768,1536]{1,0:T(8,128)} %square.1) | data formatting | bytes 9437184

commit v4 on v3

v4 whole, which is shorter than its diff:
```python
import jax
import jax.numpy as jnp
from jax import lax
from jax.experimental import pallas as pl
from jax.experimental.pallas import tpu as pltpu
from jax.sharding import PartitionSpec as P

ORB = 128
NR = 16
RB = 6
CB = 12
NB = 96
FEAT = 144
EDGES = 1024
PAIRS = RB * CB
ROWS = 768
COLS = 1536
K = 3072
NJ = 6
JW = COLS // NJ
HALF = ROWS // 2
QUART = ROWS // 4
SUB = ROWS // 8
MESH = pl.DeviceIdType.MESH


def plan():
    z_period, y_period = 12.7, 9.5
    unit_us, out_us, lag = 0.85, 2.15, 2.5
    ring = [4, 5, 0, 1, 2, 3, 7]
    events = [(0.0, "a_own", 6), (0.0, "b_own", 0), (6.0, "a_own", ring[0])]
    for j in range(NJ):
        events.append((z_period * j + 5.7, "b_relay", j))
        if j + 1 < NJ:
            events.append((z_period * j + 5.8, "b_own", j + 1))
        events.append((z_period * (j + 1) + 2.5, "b_done", j))
    events.append((17.0, "a_fwd", 6))
    for i, p in enumerate(ring):
        start = 6.3 + y_period * i
        events.append((start + 5.0, "a_relay", p))
        if i + 1 < len(ring):
            events.append((start + 5.1, "a_own", ring[i + 1]))
        else:
            events.append((start + 5.1, "a_relay", 6))
        events.append((start + 8.3, "a_fwd", p))
        events.append((start + y_period + 2.0, "a_far", p))
        events.append((start + y_period + 4.5, "a_done", p))
    last = 6.3 + y_period * len(ring)
    events.append((last + 5.0, "a_far", 6))
    events.append((last + 7.5, "a_done", 6))
    events.sort(key=lambda e: e[0])
    order = []
    now, link = 0.0, 0.0
    a_ok, b_ok = set(), set()
    arrive = {}
    todo = [(p, j) for j in range(NJ) for p in range(8)]
    ends = [(q, j) for j in range(NJ) for q in range(2)]
    done = set()
    while todo or events or ends:
        while events and events[0][0] <= now:
            _, name, arg = events.pop(0)
            order.append((name, arg))
            if name == "a_done":
                a_ok.add(arg)
            if name == "b_done":
                b_ok.add(arg)
        best = None
        wake = events[0][0] if events else 1e9
        for q, j in ends:
            if (6 + q, j) not in done or (2 + q, j) not in arrive or (4 + q, j) not in arrive:
                continue
            at = max(arrive[(2 + q, j)], arrive[(4 + q, j)])
            if at <= now:
                best = ((1, 9, j, q), ("final", q, j))
                break
            wake = min(wake, at)
        for p, j in todo:
            if p not in a_ok or j not in b_ok:
                continue
            kind, q = p // 2, p % 2
            if kind == 1:
                if (q, j) not in arrive:
                    continue
                if arrive[(q, j)] > now:
                    wake = min(wake, arrive[(q, j)])
                    continue
            rank = (2, 0, j, p) if kind == 3 else (0, kind == 1, j, p)
            if best is None or rank < best[0]:
                best = (rank, ("unit", p, j))
        if best is None:
            now = wake
            continue
        name, p, j = best[1]
        if name == "final":
            ends.remove((p, j))
            order.append(("final", p, j))
            now += 0.25
            continue
        todo.remove((p, j))
        done.add((p, j))
        last = order[-1]
        if last[0] == "unit" and last[1] == p and last[2] + last[3] == j:
            order[-1] = ("unit", p, last[2], last[3] + 1)
        else:
            order.append(("unit", p, j, 1))
        now += unit_us
        if p < 6:
            link = max(link, now) + out_us
            arrive[(p, j)] = link + lag
    return order, now


def square_kernel(
    vec_ref, atoms_ref, lower_ref, upper_ref, w_hbm, base_hbm, o_ref,
    edges, t_ref, a, b, rf, rp, rm,
    w_sem, base_sem, edge_sem, snd, rcv,
    a2_sem, al_sem, ar_sem, af_sem, sb_sem, bl_sem, br_sem, bf_sem, rf_sem, rp_sem, rm_sem,
    a2_snd, ay_snd, sb_snd, b_snd, x_snd, own_sem,
):
    row = lax.axis_index("row")
    col = lax.axis_index("col")
    z, x, y, c = row // 4, row % 4, col // 2, col % 2
    mod = lambda v: (v + 4) % 4
    dev = lambda zz, xx, yy, cc: (zz * 4 + xx, yy * 2 + cc)
    zr, zl = dev(mod(z + 1), x, y, c), dev(mod(z - 1), x, y, c)
    yr, yl = dev(z, x, mod(y + 1), c), dev(z, x, mod(y - 1), c)
    xr, xl = dev(z, mod(x + 1), y, c), dev(z, mod(x - 1), y, c)
    sib = dev(z, x, y, 1 - c)

    def build(edge_ref, padded, emb, wide, sel, w, base, direct, mirror):
        w_copy = pltpu.make_async_copy(w_hbm, w, w_sem)
        base_copy = pltpu.make_async_copy(base_hbm, base, base_sem)
        w_copy.start()
        base_copy.start()

        barrier = pltpu.get_barrier_semaphore()
        for d in range(1, 8):
            pl.semaphore_signal(
                barrier, inc=1, device_id=(row, (col + d) % 8), device_id_type=MESH
            )
        for d in range(1, 16):
            pl.semaphore_signal(
                barrier, inc=1, device_id=((row + d) % 16, col), device_id_type=MESH
            )
        for d in range(1, 4):
            pl.semaphore_signal(
                barrier, inc=1, device_id=dev(z, mod(x + d), y, 1 - c), device_id_type=MESH
            )

        padded[...] = jnp.zeros((8, ORB), jnp.float32)
        padded[0:3, 0:8] = vec_ref[...]
        padded[3:5, 0:8] = atoms_ref[...].astype(jnp.float32)
        packed = padded[0:1, :]
        for n in range(1, 5):
            packed = packed + pltpu.roll(padded[n : n + 1, :], 8 * n, 1)
        edge_ref[...] = packed
        pl.semaphore_wait(barrier, 25)

        mine = row * 8 + col
        own = pltpu.make_async_copy(edge_ref, edges.at[pl.ds(mine, 1), :], edge_sem)
        own.start()
        copies = []
        for d in range(1, 8):
            copy = pltpu.make_async_remote_copy(
                src_ref=edge_ref, dst_ref=edges.at[pl.ds(mine, 1), :],
                send_sem=snd.at[d], recv_sem=rcv.at[d],
                device_id=(row, (col + d) % 8), device_id_type=MESH,
            )
            copy.start()
            copies.append(copy)
        own.wait()
        for d in range(1, 8):
            src = row * 8 + (col + 8 - d) % 8
            pltpu.make_async_remote_copy(
                src_ref=edge_ref, dst_ref=edges.at[pl.ds(src, 1), :],
                send_sem=snd.at[d], recv_sem=rcv.at[d],
                device_id=(row, (col + d) % 8), device_id_type=MESH,
            ).wait_recv()

        def group(r):
            return edges.at[pl.ds(pl.multiple_of(r * 8, 8), 8), :]

        for d in range(1, 16):
            copy = pltpu.make_async_remote_copy(
                src_ref=group(row), dst_ref=group(row),
                send_sem=snd.at[7 + d], recv_sem=rcv.at[7 + d],
                device_id=((row + d) % 16, col), device_id_type=MESH,
            )
            copy.start()
            copies.append(copy)
        for d in range(1, 16):
            src = (row + 16 - d) % 16
            pltpu.make_async_remote_copy(
                src_ref=group(src), dst_ref=group(src),
                send_sem=snd.at[7 + d], recv_sem=rcv.at[7 + d],
                device_id=((row + d) % 16, col), device_id_type=MESH,
            ).wait_recv()
        for copy in copies:
            copy.wait_send()

        fields = edges[...].T
        vx, vy, vz = fields[0:8], fields[8:16], fields[16:24]
        first, second = fields[24:32], fields[32:40]
        radius = jnp.sqrt(vx * vx + vy * vy + vz * vz + 0.25)
        ux, uy, uz = vx / radius, vy / radius, vz / radius
        harmonics = [
            None, ux, uy, uz, ux * uy, uy * uz, uz * ux, ux * ux - uy * uy, 3.0 * uz * uz - 1.0
        ]
        for k in range(NR):
            scaled = (radius - (1.0 + 0.3 * k)) / 0.5
            radial = jnp.exp(-(scaled * scaled))
            for m in range(9):
                f = 9 * k + m
                emb[f * 8 : f * 8 + 8, :] = radial if m == 0 else radial * harmonics[m]
        number = lax.broadcasted_iota(jnp.int32, (PAIRS, ORB), 0)
        upper_atom = jnp.zeros((PAIRS, ORB), jnp.int32)
        for n in range(1, RB):
            upper_atom = upper_atom + jnp.where(number >= CB * n, 1, 0)
        pair = (row * RB + upper_atom) * NB + col * CB + number - CB * upper_atom
        pair = pair.astype(jnp.float32)
        forward = first * float(NB) + second
        backward = second * float(NB) + first
        for i in range(8):
            lanes = slice(i * ORB, (i + 1) * ORB)
            sel[0:PAIRS, lanes] = jnp.where(forward[i : i + 1] == pair, 1.0, 0.0)
            sel[PAIRS : 2 * PAIRS, lanes] = jnp.where(backward[i : i + 1] == pair, 1.0, 0.0)
            wide[:, lanes] = emb[pl.ds(i, FEAT, stride=8), :]
        coefficient = lax.dot_general(
            sel[...], wide[...], (((1,), (1,)), ((), ())),
            precision=lax.Precision.HIGHEST, preferred_element_type=jnp.float32,
        ).astype(jnp.bfloat16)

        w_copy.wait()

        def expand(n, carry):
            start = pl.multiple_of(n * 8 * ORB, 8 * ORB)
            part = jnp.dot(
                coefficient, w[:, pl.ds(start, 8 * ORB)], preferred_element_type=jnp.float32
            )
            place = pl.ds(pl.multiple_of(n * 8, 8), 8)
            direct[:, place, :] = part[:PAIRS].reshape(PAIRS, 8, ORB)
            mirror[:, place, :] = part[PAIRS:].reshape(PAIRS, 8, ORB)
            return carry

        lax.fori_loop(0, ORB // 8, expand, 0)
        base_copy.wait()
        upper = upper_ref[0]
        scale = upper - lower_ref[0]
        on_diagonal = lax.broadcasted_iota(jnp.int32, (ORB, ORB), 0) == lax.broadcasted_iota(
            jnp.int32, (ORB, ORB), 1
        )

        def finish(i, carry):
            rows = pl.ds(pl.multiple_of(i * ORB, ORB), ORB)
            for k in range(CB):
                lanes = slice(k * ORB, (k + 1) * ORB)
                both = direct[i * CB + k] + mirror[i * CB + k].T
                both = both + base[rows, lanes].astype(jnp.float32)
                shift = jnp.where(row * RB + i == col * CB + k, upper, 0.0)
                moved = jnp.where(on_diagonal, shift, 0.0) - both
                t_ref[rows, lanes] = (moved / scale).astype(jnp.bfloat16)
            return carry

        lax.fori_loop(0, RB, finish, 0)

    f32 = jnp.float32
    pl.run_scoped(
        build,
        pltpu.VMEM((1, ORB), f32),
        pltpu.VMEM((8, ORB), f32),
        pltpu.VMEM((FEAT * 8, ORB), f32),
        pltpu.VMEM((FEAT, EDGES), f32),
        pltpu.VMEM((2 * PAIRS, EDGES), f32),
        pltpu.VMEM((FEAT, ORB * ORB), jnp.bfloat16),
        pltpu.VMEM((ROWS, COLS), jnp.bfloat16),
        pltpu.VMEM((PAIRS, ORB, ORB), f32),
        pltpu.VMEM((PAIRS, ORB, ORB), f32),
    )

    pending = []

    def remote(src, dst, snd, rcv, target):
        return pltpu.make_async_remote_copy(
            src_ref=src, dst_ref=dst, send_sem=snd, recv_sem=rcv,
            device_id=target, device_id_type=MESH,
        )

    def push(src, dst, snd, rcv, target):
        copy = remote(src, dst, snd, rcv, target)
        copy.start()
        pending.append((None, copy))

    def arrived(dst, rcv):
        remote(dst, dst, own_sem.at[1], rcv, sib).wait_recv()

    def exchange(r, h, q):
        kk = mod(x - r)
        active = (kk // 2) == c
        cols = pl.ds(pl.multiple_of((kk % 2) * ROWS, ROWS), ROWS)
        place = pl.ds(pl.multiple_of(y * ROWS, ROWS), ROWS)
        p = 2 * {0: 3, 2: 0, 1: 1 + h, 3: 2 - h}[r] + q
        for s in range(2):
            src = t_ref.at[pl.ds(h * HALF + q * QUART + s * SUB, SUB), cols]
            dst = a.at[p, pl.ds(h * QUART + s * SUB, SUB), place]
            snd, rcv = a2_snd.at[r, h, q, s], a2_sem.at[p, s]
            if r:
                copy = remote(src, dst, snd, rcv, dev(z, kk, y, h))
                pl.when(active)(copy.start)
                pending.append((active, copy))
            else:
                copy = remote(src, dst, snd, rcv, sib)
                cond = active & (c != h)
                pl.when(cond)(copy.start)
                pending.append((cond, copy))
                local = pltpu.make_async_copy(src, dst, rcv)
                pl.when(active & (c == h))(local.start)

    def a_piece(p, s, yy):
        return a.at[
            p,
            pl.ds(pl.multiple_of(c * QUART + s * SUB, SUB), SUB),
            pl.ds(pl.multiple_of(yy * ROWS, ROWS), ROWS),
        ]

    def a_half(p, yy, cc):
        return a.at[
            p,
            pl.ds(pl.multiple_of(cc * QUART, QUART), QUART),
            pl.ds(pl.multiple_of(yy * ROWS, ROWS), ROWS),
        ]

    def along(p, s, yy, snd, rcv, target):
        push(a_piece(p, s, yy), a_piece(p, s, yy), ay_snd.at[p, snd], rcv.at[p, s], target)

    def share(p, i, yy):
        push(a_half(p, yy, c), a_half(p, yy, c), sb_snd.at[p, i], sb_sem.at[p, i], sib)

    def a_own(p):
        arrived(a_piece(p, 0, y), a2_sem.at[p, 0])
        along(p, 0, y, 0, al_sem, yr)
        arrived(a_piece(p, 1, y), a2_sem.at[p, 1])
        along(p, 1, y, 1, ar_sem, yl)
        along(p, 1, y, 2, al_sem, yr)
        along(p, 0, y, 3, ar_sem, yl)
        share(p, 0, y)

    def a_relay(p):
        left, right = mod(y - 1), mod(y + 1)
        arrived(a_piece(p, 0, left), al_sem.at[p, 0])
        along(p, 0, left, 4, af_sem, yr)
        arrived(a_piece(p, 1, right), ar_sem.at[p, 1])
        along(p, 1, right, 5, af_sem, yl)

    def a_fwd(p):
        left, right = mod(y - 1), mod(y + 1)
        arrived(a_piece(p, 1, left), al_sem.at[p, 1])
        if p == 6:
            arrived(a_piece(p, 0, left), al_sem.at[p, 0])
        share(p, 1, left)
        arrived(a_piece(p, 0, right), ar_sem.at[p, 0])
        if p == 6:
            arrived(a_piece(p, 1, right), ar_sem.at[p, 1])
        share(p, 2, right)

    def a_late(p):
        left, right = mod(y - 1), mod(y + 1)
        along(p, 0, left, 4, af_sem, yr)
        along(p, 1, right, 5, af_sem, yl)

    def a_far(p):
        far = mod(y + 2)
        arrived(a_piece(p, 0, far), af_sem.at[p, 0])
        arrived(a_piece(p, 1, far), af_sem.at[p, 1])
        share(p, 3, far)

    def a_done(p):
        for i, yy in enumerate((y, mod(y - 1), mod(y + 1), mod(y + 2))):
            arrived(a_half(p, yy, 1 - c), sb_sem.at[p, i])

    def b_piece(j, s, zz):
        return b.at[pl.ds(pl.multiple_of(zz * ROWS + s * HALF, HALF), HALF), pl.ds(j * JW, JW)]

    def b_own(j):
        for i, (s, right) in enumerate(((0, True), (1, False), (1, True), (0, False))):
            src = t_ref.at[pl.ds(s * HALF, HALF), pl.ds(j * JW, JW)]
            rcv = bl_sem.at[j, s] if right else br_sem.at[j, s]
            push(src, b_piece(j, s, z), b_snd.at[j, i], rcv, zr if right else zl)

    def b_relay(j):
        left, right = mod(z - 1), mod(z + 1)
        arrived(b_piece(j, 0, left), bl_sem.at[j, 0])
        push(b_piece(j, 0, left), b_piece(j, 0, left), b_snd.at[j, 4], bf_sem.at[j, 0], zr)
        arrived(b_piece(j, 1, right), br_sem.at[j, 1])
        push(b_piece(j, 1, right), b_piece(j, 1, right), b_snd.at[j, 5], bf_sem.at[j, 1], zl)

    own_tile = b.at[pl.ds(pl.multiple_of(z * ROWS, ROWS), ROWS), :]
    own_copy = pltpu.make_async_copy(t_ref, own_tile, own_sem.at[0])

    def b_done(j):
        if j == 0:
            own_copy.wait()
        arrived(b_piece(j, 1, mod(z - 1)), bl_sem.at[j, 1])
        arrived(b_piece(j, 0, mod(z + 1)), br_sem.at[j, 0])
        for s in range(2):
            arrived(b_piece(j, s, mod(z + 2)), bf_sem.at[j, s])

    def block(ref, q, h, j):
        return ref.at[pl.ds(q * HALF + h * QUART, QUART), pl.ds(j * JW, JW)]

    def unit(s0, s1, s2, out, p, first, count):
        kind, q = p // 2, p % 2
        rows = pl.ds(q * HALF, HALF)
        source = (s0, s1, s2, None)[kind]

        def step(j):
            cols = pl.ds(j * JW if count == 1 else pl.multiple_of(j * JW, JW), JW)
            if kind == 1:
                for h in range(2):
                    arrived(block(rf, q, h, j), rf_sem.at[q, h, j])
            acc = jnp.dot(a[p], b[:, cols], preferred_element_type=jnp.float32)
            if kind == 1:
                acc = acc + rf[rows, cols].astype(jnp.float32)
            if kind == 3:
                for h in range(2):
                    out[pl.ds(h * HALF + q * QUART, QUART), cols] = acc[h * QUART : (h + 1) * QUART]
                return
            source[rows, cols] = acc.astype(jnp.bfloat16)
            for h in range(2):
                reduce_copy(source, p, h, j).start()

        if count == 1:
            step(first)
        else:
            lax.fori_loop(first, first + count, lambda j, carry: (step(j), carry)[1], 0)

    def reduce_copy(source, p, h, j):
        kind, q = p // 2, p % 2
        target = xr if (h == 0) == (kind < 2) else xl
        into, sem = (rf, rf_sem) if kind == 0 else (rp, rp_sem) if target is xr else (rm, rm_sem)
        return remote(
            block(source, q, h, j), block(into, q, h, j), x_snd.at[p, h, j], sem.at[q, h, j], target
        )

    def final(out, q, j):
        cols = pl.ds(j * JW, JW)
        rows = pl.ds(q * HALF, HALF)
        for h in range(2):
            arrived(block(rp, q, h, j), rp_sem.at[q, h, j])
            arrived(block(rm, q, h, j), rm_sem.at[q, h, j])
        for h in range(2):
            rows = pl.ds(q * HALF + h * QUART, QUART)
            into = pl.ds(h * HALF + q * QUART, QUART)
            out[into, cols] = (
                out[into, cols] + rp[rows, cols].astype(jnp.float32) + rm[rows, cols].astype(jnp.float32)
            )

    def work(s0, s1, s2):
        out = o_ref
        for r, hs in ((0, (0, 1)), (1, (1,)), (3, (0,)), (2, (0, 1)), (1, (0,)), (3, (1,))):
            for q in range(2):
                for h in hs:
                    exchange(r, h, q)
        own_copy.start()
        steps = {
            "a_own": a_own, "a_relay": a_relay, "a_fwd": a_fwd, "a_far": a_far, "a_done": a_done,
            "b_own": b_own, "b_relay": b_relay, "b_done": b_done,
        }
        for name, *args in plan()[0]:
            if name == "a_relay" and args == [6]:
                a_late(6)
            elif name == "unit":
                unit(s0, s1, s2, out, *args)
            elif name == "final":
                final(out, *args)
            else:
                steps[name](*args)
        for cond, copy in pending:
            if cond is None:
                copy.wait_send()
            else:
                pl.when(cond)(copy.wait_send)
        for p in range(6):
            for h in range(2):
                for j in range(NJ):
                    reduce_copy((s0, s1, s2)[p // 2], p, h, j).wait_send()

    tiles = pltpu.VMEM((ROWS, COLS), jnp.bfloat16)
    pl.run_scoped(work, tiles, tiles, tiles)


def square(vec, atoms, lower, upper, weight, base):
    dma = pltpu.SemaphoreType.DMA
    bf = jnp.bfloat16
    return pl.pallas_call(
        square_kernel,
        out_shape=pltpu.VMEM((ROWS, COLS), jnp.float32),
        in_specs=[
            pl.BlockSpec(memory_space=pltpu.VMEM),
            pl.BlockSpec(memory_space=pltpu.VMEM),
            pl.BlockSpec(memory_space=pltpu.SMEM),
            pl.BlockSpec(memory_space=pltpu.SMEM),
            pl.BlockSpec(memory_space=pl.ANY),
            pl.BlockSpec(memory_space=pl.ANY),
        ],
        out_specs=pl.BlockSpec(memory_space=pltpu.VMEM),
        scratch_shapes=[
            pltpu.VMEM((ORB, ORB), jnp.float32),
            pltpu.VMEM((ROWS, COLS), bf),
            pltpu.VMEM((8, HALF, K), bf),
            pltpu.VMEM((K, COLS), bf),
            pltpu.VMEM((ROWS, COLS), bf),
            pltpu.VMEM((ROWS, COLS), bf),
            pltpu.VMEM((ROWS, COLS), bf),
            dma, dma, dma, dma((23,)), dma((23,)),
            dma((8, 2)), dma((8, 2)), dma((8, 2)), dma((8, 2)), dma((8, 4)),
            dma((NJ, 2)), dma((NJ, 2)), dma((NJ, 2)),
            dma((2, 2, NJ)), dma((2, 2, NJ)), dma((2, 2, NJ)),
            dma((4, 2, 2, 2)), dma((8, 6)), dma((8, 4)), dma((NJ, 6)), dma((6, 2, NJ)),
            dma((2,)),
        ],
        compiler_params=pltpu.CompilerParams(
            collective_id=0, has_side_effects=True, vmem_limit_bytes=56 * 2**20
        ),
        name="square",
    )(vec, atoms, lower, upper, weight, base)


def shards(edge_vec, edge_atoms, block_weight, base_hamiltonian, lower_bound, upper_bound):
    return square(
        edge_vec, edge_atoms, lower_bound, upper_bound, block_weight, base_hamiltonian
    )


def solution(mesh):
    return jax.shard_map(
        shards,
        mesh=mesh,
        in_specs=(P(None, ("row", "col")), P(None, ("row", "col")), P(), P("row", "col"), P(), P()),
        out_specs=P("row", "col"),
        check_vma=False,
    )
```

time: 169 us -> 144 us (0.85); the launches traced: 167 us -> 144 us
  Pallas kernels: 158 us -> 141 us
  local copies, waits for them, and re-layouts: 5.44 us -> 2.19 us
    pallas_call x2 -> x1, Pallas kernels: 158 us -> 141 us  [square(): pl.pallas_call(square_kernel, out_shape=pltpu.VMEM((ROWS, COLS), jnp.floa...]
    unnamed x1, local copies, waits for them, and re-layouts: 4.84 us -> 2.19 us
where the time goes in v4:
time: 144 us
  Pallas kernels  141 us (98%)
  local copies, waits for them, and re-layouts  2.19 us (2%)
    pallas_call x1, Pallas kernels, square(): pl.pallas_call(square_kernel, out_shape=pltpu.VMEM((ROWS, COLS), jnp.floa...  141 us

profile of v4, /device:TPU:1, one launch (start us, length us, event | category | flops | bytes accessed | tf_op | source)
XLA Modules:
  0.0 144.1 jit_solution(12616595107278513122)
XLA Ops:
  1.3 140.6 %square.1 = f32[768,1536]{1,0:T(8,128)S(1)} custom-call(f32[3,8]{1,0:T(4,128)} %vec_ref.1, s32[2,8]{1,0:T(2,128)} %atoms_ref.1, f32[1]{0:T(128)S(6)} %copy.9.lower_ref, f32[1]{0:T(128)S(6)} %copy.10.upper_ref, bf16[144,16384]{1,0:T(8,128)(2,1)} %w_hbm.1, bf16[768,1536]{1,0:T(8,128)(2,1)} %base_hbm.1), custom_call_target="tpu_custom_call" | custom-call | tf_op jit(solution)/shard_map/square/pallas_call | solution.py:494
  141.9 2.2 %copy.8 = f32[768,1536]{1,0:T(8,128)} copy(f32[768,1536]{1,0:T(8,128)S(1)} %square.1) | data formatting | bytes 9437184

commit v5 on v4

v5 whole, which is shorter than its diff:
```python
import jax
import jax.numpy as jnp
from jax import lax
from jax.experimental import pallas as pl
from jax.experimental.pallas import tpu as pltpu
from jax.sharding import PartitionSpec as P

ORB = 128
NR = 16
RB = 6
CB = 12
NB = 96
FEAT = 144
EDGES = 1024
PADDED = 40
ROWS = 768
COLS = 1536
K = 3072
NJ = 6
JW = COLS // NJ
HALF = ROWS // 2
QUART = ROWS // 4
SUB = ROWS // 8
MESH = pl.DeviceIdType.MESH


def plan():
    z_period, y_period = 12.7, 9.5
    z_lead, y_lead, x_lead = -0.5, 5.2, 24.0
    unit_us, out_us, lag = 1.05, 2.15, 3.0
    ring = [4, 5, 0, 1, 2, 3, 6, 7]
    events = [(y_lead, "a_own", ring[0])]
    for j in range(NJ):
        start = z_lead + z_period * j
        events.append((start + 5.7, "b_right", j))
        if j + 1 < NJ:
            events.append((start + 5.8, "b_own", j + 1))
        events.append((start + (10.4 if j == 0 else 5.75), "b_left", j))
        events.append((start + z_period + 2.5, "b_done", j))
    for i, p in enumerate(ring):
        start = y_lead + y_period * i
        events.append((start + 5.0, "a_relay", p))
        if i + 1 < len(ring):
            events.append((start + 5.1, "a_own", ring[i + 1]))
        events.append((start + 8.3, "a_fwd", p))
        events.append((start + y_period + 2.0, "a_far", p))
        events.append((start + y_period + 4.5, "a_done", p))
    events.sort(key=lambda e: e[0])
    order = []
    now, link = 0.0, x_lead
    a_ok, b_ok = set(), set()
    arrive = {}
    todo = [(p, j) for j in range(NJ) for p in range(8)]
    ends = [(q, j) for j in range(NJ) for q in range(2)]
    done = set()
    while todo or events or ends:
        while events and events[0][0] <= now:
            _, name, arg = events.pop(0)
            order.append((name, arg))
            if name == "a_done":
                a_ok.add(arg)
            if name == "b_done":
                b_ok.add(arg)
        best = None
        wake = events[0][0] if events else 1e9
        for q, j in ends:
            if (6 + q, j) not in done or (2 + q, j) not in arrive or (4 + q, j) not in arrive:
                continue
            at = max(arrive[(2 + q, j)], arrive[(4 + q, j)])
            if at <= now:
                best = ((1, 9, j, q), ("final", q, j))
                break
            wake = min(wake, at)
        for p, j in todo:
            if p not in a_ok or j not in b_ok:
                continue
            kind, q = p // 2, p % 2
            if kind == 1:
                if (q, j) not in arrive:
                    continue
                if arrive[(q, j)] > now:
                    wake = min(wake, arrive[(q, j)])
                    continue
            rank = (2, 0, j, p) if kind == 3 else (0, kind == 1, j, p)
            if best is None or rank < best[0]:
                best = (rank, ("unit", p, j))
        if best is None:
            now = wake
            continue
        name, p, j = best[1]
        if name == "final":
            ends.remove((p, j))
            order.append(("final", p, j))
            now += 0.25
            continue
        todo.remove((p, j))
        done.add((p, j))
        last = order[-1]
        if last[0] == "unit" and last[1] == p and last[2] + last[3] == j:
            order[-1] = ("unit", p, last[2], last[3] + 1)
        else:
            order.append(("unit", p, j, 1))
        now += unit_us
        if p < 6:
            link = max(link, now) + out_us
            arrive[(p, j)] = link + lag
    return order, now


def square_kernel(
    vec_ref, atoms_ref, lower_ref, upper_ref, w_hbm, base_hbm, o_ref,
    edges, t_ref, a, b, rf, rp, rm,
    w_sem, base_sem, edge_sem, snd, rcv,
    a2_sem, al_sem, ar_sem, af_sem, sb_sem, bl_sem, br_sem, bf_sem, rf_sem, rp_sem, rm_sem,
    a2_snd, ay_snd, sb_snd, b_snd, x_snd, own_sem,
):
    row = lax.axis_index("row")
    col = lax.axis_index("col")
    z, x, y, c = row // 4, row % 4, col // 2, col % 2
    mod = lambda v: (v + 4) % 4
    dev = lambda zz, xx, yy, cc: (zz * 4 + xx, yy * 2 + cc)
    zr, zl = dev(mod(z + 1), x, y, c), dev(mod(z - 1), x, y, c)
    yr, yl = dev(z, x, mod(y + 1), c), dev(z, x, mod(y - 1), c)
    xr, xl = dev(z, mod(x + 1), y, c), dev(z, mod(x - 1), y, c)
    sib = dev(z, x, y, 1 - c)

    pending = []

    def remote(src, dst, snd, rcv, target):
        return pltpu.make_async_remote_copy(
            src_ref=src, dst_ref=dst, send_sem=snd, recv_sem=rcv,
            device_id=target, device_id_type=MESH,
        )

    def push(src, dst, snd, rcv, target):
        copy = remote(src, dst, snd, rcv, target)
        copy.start()
        pending.append(copy)

    def arrived(dst, rcv):
        remote(dst, dst, own_sem.at[NJ], rcv, sib).wait_recv()

    def exchange(r, h, q, sent=False):
        kk = mod(x - r)
        active = (kk // 2) == c
        cols = pl.ds(pl.multiple_of((kk % 2) * ROWS, ROWS), ROWS)
        place = pl.ds(pl.multiple_of(y * ROWS, ROWS), ROWS)
        p = 2 * {0: 3, 2: 0, 1: 1 + h, 3: 2 - h}[r] + q
        for s in range(2):
            src = t_ref.at[pl.ds(h * HALF + q * QUART + s * SUB, SUB), cols]
            dst = a.at[p, pl.ds(h * QUART + s * SUB, SUB), place]
            snd, rcv = a2_snd.at[r, h, q, s], a2_sem.at[p, s]
            if r:
                copy = remote(src, dst, snd, rcv, dev(z, kk, y, h))
                pl.when(active)(copy.wait_send if sent else copy.start)
            else:
                copy = remote(src, dst, snd, rcv, sib)
                pl.when(active & (c != h))(copy.wait_send if sent else copy.start)
                if not sent:
                    local = pltpu.make_async_copy(src, dst, rcv)
                    pl.when(active & (c == h))(local.start)

    def a_piece(p, s, yy):
        return a.at[
            p,
            pl.ds(pl.multiple_of(c * QUART + s * SUB, SUB), SUB),
            pl.ds(pl.multiple_of(yy * ROWS, ROWS), ROWS),
        ]

    def a_half(p, yy, cc):
        return a.at[
            p,
            pl.ds(pl.multiple_of(cc * QUART, QUART), QUART),
            pl.ds(pl.multiple_of(yy * ROWS, ROWS), ROWS),
        ]

    def along(p, s, yy, snd, rcv, target):
        push(a_piece(p, s, yy), a_piece(p, s, yy), ay_snd.at[p, snd], rcv.at[p, s], target)

    def share(p, i, yy):
        push(a_half(p, yy, c), a_half(p, yy, c), sb_snd.at[p, i], sb_sem.at[p, i], sib)

    def a_own(p):
        arrived(a_piece(p, 0, y), a2_sem.at[p, 0])
        along(p, 0, y, 0, al_sem, yr)
        arrived(a_piece(p, 1, y), a2_sem.at[p, 1])
        along(p, 1, y, 1, ar_sem, yl)
        along(p, 1, y, 2, al_sem, yr)
        along(p, 0, y, 3, ar_sem, yl)
        share(p, 0, y)

    def a_relay(p):
        left, right = mod(y - 1), mod(y + 1)
        arrived(a_piece(p, 0, left), al_sem.at[p, 0])
        along(p, 0, left, 4, af_sem, yr)
        arrived(a_piece(p, 1, right), ar_sem.at[p, 1])
        along(p, 1, right, 5, af_sem, yl)

    def a_fwd(p):
        left, right = mod(y - 1), mod(y + 1)
        arrived(a_piece(p, 1, left), al_sem.at[p, 1])
        share(p, 1, left)
        arrived(a_piece(p, 0, right), ar_sem.at[p, 0])
        share(p, 2, right)

    def a_far(p):
        far = mod(y + 2)
        arrived(a_piece(p, 0, far), af_sem.at[p, 0])
        arrived(a_piece(p, 1, far), af_sem.at[p, 1])
        share(p, 3, far)

    def a_done(p):
        for i, yy in enumerate((y, mod(y - 1), mod(y + 1), mod(y + 2))):
            arrived(a_half(p, yy, 1 - c), sb_sem.at[p, i])

    def b_piece(j, s, zz):
        return b.at[j, pl.ds(pl.multiple_of(zz * ROWS + s * HALF, HALF), HALF), :]

    def b_send(j, s, right, sent=False):
        src = t_ref.at[pl.ds(s * HALF, HALF), pl.ds(j * JW, JW)]
        rcv = bl_sem.at[j, s] if right else br_sem.at[j, s]
        copy = remote(src, b_piece(j, s, z), b_snd.at[j, 2 * s + right], rcv, zr if right else zl)
        (copy.wait_send if sent else copy.start)()

    def b_own(j):
        for s, right in ((0, True), (1, False), (1, True), (0, False)):
            b_send(j, s, right)

    def b_right(j):
        left = mod(z - 1)
        arrived(b_piece(j, 0, left), bl_sem.at[j, 0])
        push(b_piece(j, 0, left), b_piece(j, 0, left), b_snd.at[j, 4], bf_sem.at[j, 0], zr)

    def b_left(j):
        right = mod(z + 1)
        arrived(b_piece(j, 1, right), br_sem.at[j, 1])
        push(b_piece(j, 1, right), b_piece(j, 1, right), b_snd.at[j, 5], bf_sem.at[j, 1], zl)

    def own_copy(j):
        rows = pl.ds(pl.multiple_of(z * ROWS, ROWS), ROWS)
        return pltpu.make_async_copy(t_ref.at[:, pl.ds(j * JW, JW)], b.at[j, rows, :], own_sem.at[j])

    def b_done(j):
        own_copy(j).wait()
        arrived(b_piece(j, 1, mod(z - 1)), bl_sem.at[j, 1])
        arrived(b_piece(j, 0, mod(z + 1)), br_sem.at[j, 0])
        for s in range(2):
            arrived(b_piece(j, s, mod(z + 2)), bf_sem.at[j, s])

    def block(ref, q, h, j):
        return ref.at[j, pl.ds(q * HALF + h * QUART, QUART), :]

    def unit(s0, s1, s2, out, p, first, count):
        kind, q = p // 2, p % 2
        rows = pl.ds(q * HALF, HALF)
        source = (s0, s1, s2, None)[kind]

        def step(j):
            cols = pl.ds(j * JW if count == 1 else pl.multiple_of(j * JW, JW), JW)
            if kind == 1:
                for h in range(2):
                    arrived(block(rf, q, h, j), rf_sem.at[q, h, j])
            acc = jnp.dot(a[p], b[j], preferred_element_type=jnp.float32)
            if kind == 1:
                acc = acc + rf[j, rows, :].astype(jnp.float32)
            if kind == 3:
                for h in range(2):
                    out[pl.ds(h * HALF + q * QUART, QUART), cols] = acc[h * QUART : (h + 1) * QUART]
                return
            source[j, rows, :] = acc.astype(jnp.bfloat16)
            for h in range(2):
                reduce_copy(source, p, h, j).start()

        if count == 1:
            step(first)
        else:
            lax.fori_loop(first, first + count, lambda j, carry: (step(j), carry)[1], 0)

    def reduce_copy(source, p, h, j):
        kind, q = p // 2, p % 2
        target = xr if (h == 0) == (kind < 2) else xl
        into, sem = (rf, rf_sem) if kind == 0 else (rp, rp_sem) if target is xr else (rm, rm_sem)
        return remote(
            block(source, q, h, j), block(into, q, h, j), x_snd.at[p, h, j], sem.at[q, h, j], target
        )

    def final(out, q, j):
        cols = pl.ds(j * JW, JW)
        rows = pl.ds(q * HALF, HALF)
        for h in range(2):
            arrived(block(rp, q, h, j), rp_sem.at[q, h, j])
            arrived(block(rm, q, h, j), rm_sem.at[q, h, j])
        for h in range(2):
            rows = pl.ds(q * HALF + h * QUART, QUART)
            into = pl.ds(h * HALF + q * QUART, QUART)
            out[into, cols] = (
                out[into, cols] + rp[j, rows, :].astype(jnp.float32) + rm[j, rows, :].astype(jnp.float32)
            )

    def build(edge_ref, padded, emb, wide, sel, w, base, direct, mirror):
        w_copy = pltpu.make_async_copy(w_hbm, w, w_sem)
        base_copy = pltpu.make_async_copy(base_hbm, base, base_sem)
        w_copy.start()
        base_copy.start()

        barrier = pltpu.get_barrier_semaphore()
        for d in range(1, 8):
            pl.semaphore_signal(
                barrier, inc=1, device_id=(row, (col + d) % 8), device_id_type=MESH
            )
        for d in range(1, 16):
            pl.semaphore_signal(
                barrier, inc=1, device_id=((row + d) % 16, col), device_id_type=MESH
            )
        for d in range(1, 4):
            pl.semaphore_signal(
                barrier, inc=1, device_id=dev(z, mod(x + d), y, 1 - c), device_id_type=MESH
            )

        padded[...] = jnp.zeros((8, ORB), jnp.float32)
        padded[0:3, 0:8] = vec_ref[...]
        padded[3:5, 0:8] = atoms_ref[...].astype(jnp.float32)
        packed = padded[0:1, :]
        for n in range(1, 5):
            packed = packed + pltpu.roll(padded[n : n + 1, :], 8 * n, 1)
        edge_ref[...] = packed
        pl.semaphore_wait(barrier, 25)

        mine = row * 8 + col
        own = pltpu.make_async_copy(edge_ref, edges.at[pl.ds(mine, 1), :], edge_sem)
        own.start()
        copies = []
        for d in range(1, 8):
            copy = pltpu.make_async_remote_copy(
                src_ref=edge_ref, dst_ref=edges.at[pl.ds(mine, 1), :],
                send_sem=snd.at[d], recv_sem=rcv.at[d],
                device_id=(row, (col + d) % 8), device_id_type=MESH,
            )
            copy.start()
            copies.append(copy)
        own.wait()
        for d in range(1, 8):
            src = row * 8 + (col + 8 - d) % 8
            pltpu.make_async_remote_copy(
                src_ref=edge_ref, dst_ref=edges.at[pl.ds(src, 1), :],
                send_sem=snd.at[d], recv_sem=rcv.at[d],
                device_id=(row, (col + d) % 8), device_id_type=MESH,
            ).wait_recv()

        def group(r):
            return edges.at[pl.ds(pl.multiple_of(r * 8, 8), 8), :]

        for d in range(1, 16):
            copy = pltpu.make_async_remote_copy(
                src_ref=group(row), dst_ref=group(row),
                send_sem=snd.at[7 + d], recv_sem=rcv.at[7 + d],
                device_id=((row + d) % 16, col), device_id_type=MESH,
            )
            copy.start()
            copies.append(copy)
        for d in range(1, 16):
            src = (row + 16 - d) % 16
            pltpu.make_async_remote_copy(
                src_ref=group(src), dst_ref=group(src),
                send_sem=snd.at[7 + d], recv_sem=rcv.at[7 + d],
                device_id=((row + d) % 16, col), device_id_type=MESH,
            ).wait_recv()
        for copy in copies:
            copy.wait_send()

        fields = edges[...].T
        vx, vy, vz = fields[0:8], fields[8:16], fields[16:24]
        first, second = fields[24:32], fields[32:40]
        radius = jnp.sqrt(vx * vx + vy * vy + vz * vz + 0.25)
        ux, uy, uz = vx / radius, vy / radius, vz / radius
        harmonics = [
            None, ux, uy, uz, ux * uy, uy * uz, uz * ux, ux * ux - uy * uy, 3.0 * uz * uz - 1.0
        ]
        for k in range(NR):
            scaled = (radius - (1.0 + 0.3 * k)) / 0.5
            radial = jnp.exp(-(scaled * scaled))
            for m in range(9):
                f = 9 * k + m
                emb[f * 8 : f * 8 + 8, :] = radial if m == 0 else radial * harmonics[m]
        number = lax.broadcasted_iota(jnp.int32, (PADDED, ORB), 0)
        upper_atom = jnp.zeros((PADDED, ORB), jnp.int32)
        for n in range(1, RB):
            upper_atom = upper_atom + jnp.where(number >= CB * n, 1, 0)
        pair = (row * RB + upper_atom) * NB + col * CB + number - CB * upper_atom
        pair = pair.astype(jnp.float32)
        forward = first * float(NB) + second
        backward = second * float(NB) + first
        for i in range(8):
            lanes = slice(i * ORB, (i + 1) * ORB)
            for h in range(2):
                wanted = pair + float(h * RB // 2 * NB)
                at = 2 * PADDED * h
                sel[at : at + PADDED, lanes] = jnp.where(forward[i : i + 1] == wanted, 1.0, 0.0)
                sel[at + PADDED : at + 2 * PADDED, lanes] = jnp.where(
                    backward[i : i + 1] == wanted, 1.0, 0.0
                )
            wide[:, lanes] = emb[pl.ds(i, FEAT, stride=8), :]
        coefficient = lax.dot_general(
            sel[...], wide[...], (((1,), (1,)), ((), ())),
            precision=lax.Precision.HIGHEST, preferred_element_type=jnp.float32,
        ).astype(jnp.bfloat16)

        w_copy.wait()

        base_copy.wait()
        upper = upper_ref[0]
        scale = upper - lower_ref[0]
        on_diagonal = lax.broadcasted_iota(jnp.int32, (ORB, ORB), 0) == lax.broadcasted_iota(
            jnp.int32, (ORB, ORB), 1
        )

        def expand(n, carry):
            start = pl.multiple_of(n * 8 * ORB, 8 * ORB)
            part = jnp.dot(
                coefficient, w[:, pl.ds(start, 8 * ORB)], preferred_element_type=jnp.float32
            )
            place = pl.ds(pl.multiple_of(n * 8, 8), 8)
            for h in range(2):
                at = 2 * PADDED * h
                direct[h, :, place, :] = part[at : at + PADDED].reshape(PADDED, 8, ORB)
                at = at + PADDED
                mirror[h, :, place, :] = part[at : at + PADDED].reshape(PADDED, 8, ORB)
            return carry

        lax.fori_loop(0, ORB // 8, expand, 0)
        inverse = 1.0 / scale

        def half_tile(h):
            def finish(i, carry):
                rows = pl.ds(pl.multiple_of(h * HALF + i * ORB, ORB), ORB)
                for k in range(CB):
                    lanes = slice(k * ORB, (k + 1) * ORB)
                    both = direct[h, i * CB + k] + mirror[h, i * CB + k].T
                    both = both + base[rows, lanes].astype(jnp.float32)
                    atom = row * RB + h * (RB // 2) + i
                    shift = jnp.where(atom == col * CB + k, upper, 0.0)
                    moved = jnp.where(on_diagonal, shift, 0.0) - both
                    t_ref[rows, lanes] = (moved * inverse).astype(jnp.bfloat16)
                return carry

            lax.fori_loop(0, RB // 2, finish, 0)

        half_tile(0)
        for r, h, q in ((3, 0, 0), (3, 0, 1), (2, 0, 0)):
            exchange(r, h, q)
        b_send(0, 0, True)
        b_send(0, 0, False)
        for q in range(2):
            exchange(0, 0, q)
        half_tile(1)
        for r, h, q in (
            (1, 1, 0), (1, 1, 1), (2, 1, 0), (2, 0, 1), (2, 1, 1),
            (1, 0, 0), (3, 1, 0), (1, 0, 1), (3, 1, 1),
        ):
            exchange(r, h, q)
        b_send(0, 1, True)
        b_send(0, 1, False)
        for q in range(2):
            exchange(0, 1, q)

    f32 = jnp.float32
    pl.run_scoped(
        build,
        pltpu.VMEM((1, ORB), f32),
        pltpu.VMEM((8, ORB), f32),
        pltpu.VMEM((FEAT * 8, ORB), f32),
        pltpu.VMEM((FEAT, EDGES), f32),
        pltpu.VMEM((4 * PADDED, EDGES), f32),
        pltpu.VMEM((FEAT, ORB * ORB), jnp.bfloat16),
        pltpu.VMEM((ROWS, COLS), jnp.bfloat16),
        pltpu.VMEM((2, PADDED, ORB, ORB), f32),
        pltpu.VMEM((2, PADDED, ORB, ORB), f32),
    )

    def work(s0, s1, s2):
        out = o_ref
        for j in range(NJ):
            own_copy(j).start()
        steps = {
            "a_own": a_own, "a_relay": a_relay, "a_fwd": a_fwd, "a_far": a_far, "a_done": a_done,
            "b_own": b_own, "b_right": b_right, "b_left": b_left, "b_done": b_done,
        }
        for name, *args in plan()[0]:
            if name == "unit":
                unit(s0, s1, s2, out, *args)
            elif name == "final":
                final(out, *args)
            else:
                steps[name](*args)
        for copy in pending:
            copy.wait_send()
        for i in range(16):
            exchange(i // 4, i // 2 % 2, i % 2, True)
        for i in range(4 * NJ):
            b_send(i // 4, i // 2 % 2, i % 2 == 0, True)
        for p in range(6):
            for h in range(2):
                for j in range(NJ):
                    reduce_copy((s0, s1, s2)[p // 2], p, h, j).wait_send()

    tiles = pltpu.VMEM((NJ, ROWS, JW), jnp.bfloat16)
    pl.run_scoped(work, tiles, tiles, tiles)


def square(vec, atoms, lower, upper, weight, base):
    dma = pltpu.SemaphoreType.DMA
    bf = jnp.bfloat16
    return pl.pallas_call(
        square_kernel,
        out_shape=pltpu.VMEM((ROWS, COLS), jnp.float32),
        in_specs=[
            pl.BlockSpec(memory_space=pltpu.VMEM),
            pl.BlockSpec(memory_space=pltpu.VMEM),
            pl.BlockSpec(memory_space=pltpu.SMEM),
            pl.BlockSpec(memory_space=pltpu.SMEM),
            pl.BlockSpec(memory_space=pl.ANY),
            pl.BlockSpec(memory_space=pl.ANY),
        ],
        out_specs=pl.BlockSpec(memory_space=pltpu.VMEM),
        scratch_shapes=[
            pltpu.VMEM((ORB, ORB), jnp.float32),
            pltpu.VMEM((ROWS, COLS), bf),
            pltpu.VMEM((8, HALF, K), bf),
            pltpu.VMEM((NJ, K, JW), bf),
            pltpu.VMEM((NJ, ROWS, JW), bf),
            pltpu.VMEM((NJ, ROWS, JW), bf),
            pltpu.VMEM((NJ, ROWS, JW), bf),
            dma, dma, dma, dma((23,)), dma((23,)),
            dma((8, 2)), dma((8, 2)), dma((8, 2)), dma((8, 2)), dma((8, 4)),
            dma((NJ, 2)), dma((NJ, 2)), dma((NJ, 2)),
            dma((2, 2, NJ)), dma((2, 2, NJ)), dma((2, 2, NJ)),
            dma((4, 2, 2, 2)), dma((8, 6)), dma((8, 4)), dma((NJ, 6)), dma((6, 2, NJ)),
            dma((NJ + 1,)),
        ],
        compiler_params=pltpu.CompilerParams(
            collective_id=0, has_side_effects=True, vmem_limit_bytes=56 * 2**20
        ),
        name="square",
    )(vec, atoms, lower, upper, weight, base)


def shards(edge_vec, edge_atoms, block_weight, base_hamiltonian, lower_bound, upper_bound):
    return square(
        edge_vec, edge_atoms, lower_bound, upper_bound, block_weight, base_hamiltonian
    )


def solution(mesh):
    return jax.shard_map(
        shards,
        mesh=mesh,
        in_specs=(P(None, ("row", "col")), P(None, ("row", "col")), P(), P("row", "col"), P(), P()),
        out_specs=P("row", "col"),
        check_vma=False,
    )
```

time: 144 us -> 145 us (level)
  no operation moved by 1% of the time
where the time goes in v5:
time: 145 us
  Pallas kernels  141 us (97%)
  local copies, waits for them, and re-layouts  2.19 us (2%)
    pallas_call x1, Pallas kernels, square(): pl.pallas_call(square_kernel, out_shape=pltpu.VMEM((ROWS, COLS), jnp.floa...  141 us

profile of v5, /device:TPU:1, one launch (start us, length us, event | category | flops | bytes accessed | tf_op | source)
XLA Modules:
  0.0 144.8 jit_solution(10428584471108734969)
XLA Ops:
  1.3 141.3 %square.1 = f32[768,1536]{1,0:T(8,128)S(1)} custom-call(f32[3,8]{1,0:T(4,128)} %vec_ref.1, s32[2,8]{1,0:T(2,128)} %atoms_ref.1, f32[1]{0:T(128)S(6)} %copy.9.lower_ref, f32[1]{0:T(128)S(6)} %copy.10.upper_ref, bf16[144,16384]{1,0:T(8,128)(2,1)} %w_hbm.1, bf16[768,1536]{1,0:T(8,128)(2,1)} %base_hbm.1), custom_call_target="tpu_custom_call" | custom-call | tf_op jit(solution)/shard_map/square/pallas_call | solution.py:513
  142.6 2.2 %copy.8 = f32[768,1536]{1,0:T(8,128)} copy(f32[768,1536]{1,0:T(8,128)S(1)} %square.1) | data formatting | bytes 9437184

commit v6 on v5

--- a/solution.py
+++ b/solution.py
@@ -22,6 +22,9 @@
 QUART = ROWS // 4
 SUB = ROWS // 8
 MESH = pl.DeviceIdType.MESH
+HOPS = (0, 1, 2, 1)
+COL_ORDER = sorted(range(1, 8), key=lambda d: -HOPS[d // 2])
+ROW_ORDER = sorted(range(1, 16), key=lambda d: -HOPS[d // 4] - HOPS[d % 4])
 
 
 def plan():
@@ -304,11 +307,7 @@
         base_copy.start()
 
         barrier = pltpu.get_barrier_semaphore()
-        for d in range(1, 8):
-            pl.semaphore_signal(
-                barrier, inc=1, device_id=(row, (col + d) % 8), device_id_type=MESH
-            )
-        for d in range(1, 16):
+        for d in ROW_ORDER:
             pl.semaphore_signal(
                 barrier, inc=1, device_id=((row + d) % 16, col), device_id_type=MESH
             )
@@ -316,7 +315,10 @@
             pl.semaphore_signal(
                 barrier, inc=1, device_id=dev(z, mod(x + d), y, 1 - c), device_id_type=MESH
             )
-
+        for d in COL_ORDER:
+            pl.semaphore_signal(
+                barrier, inc=1, device_id=(row, (col + d) % 8), device_id_type=MESH
+            )
         padded[...] = jnp.zeros((8, ORB), jnp.float32)
         padded[0:3, 0:8] = vec_ref[...]
         padded[3:5, 0:8] = atoms_ref[...].astype(jnp.float32)
@@ -330,7 +332,7 @@
         own = pltpu.make_async_copy(edge_ref, edges.at[pl.ds(mine, 1), :], edge_sem)
         own.start()
         copies = []
-        for d in range(1, 8):
+        for d in COL_ORDER:
             copy = pltpu.make_async_remote_copy(
                 src_ref=edge_ref, dst_ref=edges.at[pl.ds(mine, 1), :],
                 send_sem=snd.at[d], recv_sem=rcv.at[d],
@@ -339,7 +341,7 @@
             copy.start()
             copies.append(copy)
         own.wait()
-        for d in range(1, 8):
+        for d in COL_ORDER:
             src = row * 8 + (col + 8 - d) % 8
             pltpu.make_async_remote_copy(
                 src_ref=edge_ref, dst_ref=edges.at[pl.ds(src, 1), :],
@@ -350,7 +352,7 @@
         def group(r):
             return edges.at[pl.ds(pl.multiple_of(r * 8, 8), 8), :]
 
-        for d in range(1, 16):
+        for d in ROW_ORDER:
             copy = pltpu.make_async_remote_copy(
                 src_ref=group(row), dst_ref=group(row),
                 send_sem=snd.at[7 + d], recv_sem=rcv.at[7 + d],
@@ -358,15 +360,13 @@
             )
             copy.start()
             copies.append(copy)
-        for d in range(1, 16):
+        for d in ROW_ORDER:
             src = (row + 16 - d) % 16
             pltpu.make_async_remote_copy(
                 src_ref=group(src), dst_ref=group(src),
                 send_sem=snd.at[7 + d], recv_sem=rcv.at[7 + d],
                 device_id=((row + d) % 16, col), device_id_type=MESH,
             ).wait_recv()
-        for copy in copies:
-            copy.wait_send()
 
         fields = edges[...].T
         vx, vy, vz = fields[0:8], fields[8:16], fields[16:24]
@@ -405,6 +405,8 @@
             precision=lax.Precision.HIGHEST, preferred_element_type=jnp.float32,
         ).astype(jnp.bfloat16)
 
+        for copy in copies:
+            copy.wait_send()
         w_copy.wait()
 
         base_copy.wait()

time: 145 us -> 145 us (level)
  no operation moved by 1% of the time
where the time goes in v6:
time: 145 us
  Pallas kernels  142 us (98%)
  local copies, waits for them, and re-layouts  2.19 us (2%)
    pallas_call x1, Pallas kernels, square(): pl.pallas_call(square_kernel, out_shape=pltpu.VMEM((ROWS, COLS), jnp.floa...  142 us

profile of v6, /device:TPU:1, one launch (start us, length us, event | category | flops | bytes accessed | tf_op | source)
XLA Modules:
  0.0 145.1 jit_solution(7079492827528045778)
XLA Ops:
  1.3 141.6 %square.1 = f32[768,1536]{1,0:T(8,128)S(1)} custom-call(f32[3,8]{1,0:T(4,128)} %vec_ref.1, s32[2,8]{1,0:T(2,128)} %atoms_ref.1, f32[1]{0:T(128)S(6)} %copy.9.lower_ref, f32[1]{0:T(128)S(6)} %copy.10.upper_ref, bf16[144,16384]{1,0:T(8,128)(2,1)} %w_hbm.1, bf16[768,1536]{1,0:T(8,128)(2,1)} %base_hbm.1), custom_call_target="tpu_custom_call" | custom-call | tf_op jit(solution)/shard_map/square/pallas_call | solution.py:515
  142.9 2.2 %copy.8 = f32[768,1536]{1,0:T(8,128)} copy(f32[768,1536]{1,0:T(8,128)S(1)} %square.1) | data formatting | bytes 9437184
